TPU v7x, 32 devices: a whole 2x2x4 slice. The times are simulated.
32 devices in a mesh: parts: 32 (over z, y, x, core).
Axes of the slice: x: 2, y: 2, z: 4, core: 2. Of those that a mesh axis runs over, the one named last changes fastest.
Arguments:
- rhs: float32 [216, 16384], P(None, 'parts'), may hold values from -60 to 90
- start: float32 [216, 16384], P(None, 'parts'), may hold values from -3.75 to 5.625
- spectrum_top: float32 [1], replicated, may hold values from 10 to 20
- elem_code: int32 [16384], P('parts'), may hold values from 0 to 2, as said below
- rec_elem: int32 [98304], P('parts'), may hold values from 0 to 511, as said below
- rec_dir: int32 [98304], P('parts'), may hold values from 0 to 5
- rec_sub: int32 [98304], P('parts'), may hold values from 0 to 5, as said below
- rec_peer: int32 [98304], P('parts'), may hold values from -1 to 31, as said below
- rec_index: int32 [98304], P('parts'), may hold values from 0 to 3071, as said below
- send_rec: int32 [262144], P('parts'), may hold values from 0 to 3071, as said below
Outputs:
- solution: float32 [216, 16384], P(None, 'parts')
- norms: float32 [3, 2], replicated
Inputs may be any that keep to these rules, and one draw needn't show every extreme that they name: `elem_code`: 0 marks an empty slot, 1 a fine element, 2 a coarse element; a device's live slots come first. `rec_elem`: always a live element of the record's device. `rec_sub`: 0 to 3: a quarter of a coarse face facing a fine element; 4: the whole face; 5: an unused slot, which comes after the device's used records. `rec_peer`: -1 at the channel's ends and on unused slots. A partner is never more than 7 devices away; its face has the opposite direction, and the partner's partner is the record itself. `rec_index`: A record index on the same device, or a slot of the partner device's send list to this device. `send_rec`: entries of slots that no record names are arbitrary. At most 256 slots are named from one device to another, and some pair of devices uses all 256.
All inputs are finite; a program needn't handle non-finite values.
Results may differ from a plain program's by a relative error of at most 0.0003.
Values sent between devices are 32-bit elements; how exact they have to be, the bound alone decides.
A program may use at most 128 MiB of HBM per device.

v0:
```python
import math

import jax
import jax.numpy as jnp
import numpy as np
from jax import lax
from jax.sharding import PartitionSpec as P

LD = 4
ITERS = 3


PENALTY = 36.0
BOTTOM_RATIO = 8.0
HIGHEST = lax.Precision.HIGHEST


def shifted(shard, axis, by):
    size = lax.axis_size(axis)
    pairs = [(i, i + by) for i in range(size) if 0 <= i + by < size]
    return lax.ppermute(shard, axis, pairs)


def lobatto_tables():
    root_seven = math.sqrt(7.0)
    inner_root = math.sqrt(1.0 / 3.0 - 2.0 * root_seven / 21.0)
    outer_root = math.sqrt(1.0 / 3.0 + 2.0 * root_seven / 21.0)
    points = (np.array([-1.0, -outer_root, -inner_root, inner_root, outer_root, 1.0]) + 1.0) / 2.0
    weights = (
        np.array(
            [
                1.0 / 15.0,
                (14.0 - root_seven) / 30.0,
                (14.0 + root_seven) / 30.0,
                (14.0 + root_seven) / 30.0,
                (14.0 - root_seven) / 30.0,
                1.0 / 15.0,
            ]
        )
        / 2.0
    )
    barycentric = np.array(
        [1.0 / np.prod([points[j] - points[k] for k in range(6) if k != j]) for j in range(6)]
    )
    derivative = np.zeros((6, 6))
    for i in range(6):
        for j in range(6):
            if i != j:
                derivative[i, j] = barycentric[j] / barycentric[i] / (points[i] - points[j])
        derivative[i, i] = -np.sum(derivative[i])
    halves = np.zeros((2, 6, 6))
    for which_half in range(2):
        targets = (points + which_half) / 2.0
        for i in range(6):
            for j in range(6):
                halves[which_half, i, j] = np.prod(
                    [(targets[i] - points[k]) / (points[j] - points[k]) for k in range(6) if k != j]
                )
    column_sums = np.sum(derivative * derivative * weights[:, None], axis=0)
    stiff_diag = (
        column_sums[:, None, None] * weights[None, :, None] * weights[None, None, :]
        + weights[:, None, None] * column_sums[None, :, None] * weights[None, None, :]
        + weights[:, None, None] * weights[None, :, None] * column_sums[None, None, :]
    )
    return (weights, derivative, halves, stiff_diag.reshape(216))


def float_tables():
    weights, derivative, halves, stiff_diag = lobatto_tables()
    return (
        jnp.asarray(weights, dtype=jnp.float32),
        jnp.asarray(derivative, dtype=jnp.float32),
        jnp.asarray(halves, dtype=jnp.float32),
        jnp.asarray(stiff_diag, dtype=jnp.float32),
    )


def face_traces(nodal_field, inv_size, derivative):
    values = []
    normals = []
    for direction in range(6):
        axis_index = direction // 2
        layer_index = 5 * (direction % 2)
        orientation = 2.0 * (direction % 2) - 1.0
        slope_row = derivative[layer_index]
        if axis_index == 0:
            face_value = nodal_field[layer_index]
            normal = jnp.einsum("m,mjke->jke", slope_row, nodal_field, precision=HIGHEST)
        elif axis_index == 1:
            face_value = nodal_field[:, layer_index]
            normal = jnp.einsum("m,imke->ike", slope_row, nodal_field, precision=HIGHEST)
        else:
            face_value = nodal_field[:, :, layer_index]
            normal = jnp.einsum("m,ijme->ije", slope_row, nodal_field, precision=HIGHEST)
        values.append(face_value.reshape(36, -1))
        normals.append((normal * (orientation * inv_size)).reshape(36, -1))
    return (jnp.concatenate(values, axis=1), jnp.concatenate(normals, axis=1))


def lift_faces(face_value, face_slope, inv_size, derivative, elem_count):
    result = jnp.zeros((6, 6, 6, elem_count), jnp.float32)
    for direction in range(6):
        axis_index = direction // 2
        layer_index = 5 * (direction % 2)
        orientation = 2.0 * (direction % 2) - 1.0
        slope_row = derivative[layer_index]
        part_value = face_value[:, direction * elem_count : (direction + 1) * elem_count].reshape(
            6, 6, elem_count
        )
        part_slope = face_slope[:, direction * elem_count : (direction + 1) * elem_count].reshape(
            6, 6, elem_count
        )
        part_slope = part_slope * (orientation * inv_size)
        if axis_index == 0:
            result = result.at[layer_index].add(part_value)
            result = result + jnp.einsum("m,jke->mjke", slope_row, part_slope, precision=HIGHEST)
        elif axis_index == 1:
            result = result.at[:, layer_index].add(part_value)
            result = result + jnp.einsum("m,ike->imke", slope_row, part_slope, precision=HIGHEST)
        else:
            result = result.at[:, :, layer_index].add(part_value)
            result = result + jnp.einsum("m,ije->ijme", slope_row, part_slope, precision=HIGHEST)
    return result


def volume_term(nodal_field, elem_size, weight_cube, derivative):
    cube_scale = weight_cube[:, :, :, None] * elem_size
    grad_x = jnp.einsum("im,mjke->ijke", derivative, nodal_field, precision=HIGHEST) * cube_scale
    grad_y = jnp.einsum("jm,imke->ijke", derivative, nodal_field, precision=HIGHEST) * cube_scale
    grad_z = jnp.einsum("km,ijme->ijke", derivative, nodal_field, precision=HIGHEST) * cube_scale
    result = jnp.einsum("mi,mjke->ijke", derivative, grad_x, precision=HIGHEST)
    result = result + jnp.einsum("mj,imke->ijke", derivative, grad_y, precision=HIGHEST)
    return result + jnp.einsum("mk,ijme->ijke", derivative, grad_z, precision=HIGHEST)


def onto_both(face_nodes, rec_sub, halves):
    whole_face = rec_sub >= 4
    first_bit = rec_sub % 2
    second_bit = rec_sub // 2 % 2
    lower_half = jnp.einsum("ij,pjkr->pikr", halves[0], face_nodes, precision=HIGHEST)
    upper_half = jnp.einsum("ij,pjkr->pikr", halves[1], face_nodes, precision=HIGHEST)
    face_nodes = jnp.where(
        whole_face, face_nodes, jnp.where(first_bit == 0, lower_half, upper_half)
    )
    lower_half = jnp.einsum("kj,pijr->pikr", halves[0], face_nodes, precision=HIGHEST)
    upper_half = jnp.einsum("kj,pijr->pikr", halves[1], face_nodes, precision=HIGHEST)
    return jnp.where(whole_face, face_nodes, jnp.where(second_bit == 0, lower_half, upper_half))


def off_both(face_nodes, rec_sub, halves):
    whole_face = rec_sub >= 4
    first_bit = rec_sub % 2
    second_bit = rec_sub // 2 % 2
    lower_half = jnp.einsum("jk,pijr->pikr", halves[0], face_nodes, precision=HIGHEST)
    upper_half = jnp.einsum("jk,pijr->pikr", halves[1], face_nodes, precision=HIGHEST)
    face_nodes = jnp.where(
        whole_face, face_nodes, jnp.where(second_bit == 0, lower_half, upper_half)
    )
    lower_half = jnp.einsum("ji,pjkr->pikr", halves[0], face_nodes, precision=HIGHEST)
    upper_half = jnp.einsum("ji,pjkr->pikr", halves[1], face_nodes, precision=HIGHEST)
    return jnp.where(whole_face, face_nodes, jnp.where(first_bit == 0, lower_half, upper_half))


def mortar_terms(own_traces, partner, is_bound, mortar_size, live_rec, face_weight):
    own_value = own_traces[:36]
    own_slope = own_traces[36:]
    part_value = jnp.where(is_bound, 0.0, partner[:36])
    part_slope = jnp.where(is_bound, -own_slope, partner[36:])
    jump_value = own_value - part_value
    flux_value = 0.5 * (own_slope - part_slope)
    adjoint = jnp.where(is_bound, 1.0, 0.5)
    area_scale = mortar_size * mortar_size
    weight_live = face_weight[:, None] * live_rec
    term_value = weight_live * (PENALTY * mortar_size * jump_value - area_scale * flux_value)
    term_slope = -weight_live * adjoint * area_scale * jump_value
    return (term_value, term_slope)


def on_device(
    rhs, start, spectrum_top, elem_code, rec_elem, rec_dir, rec_sub, rec_peer, rec_index, send_rec
):
    weights, derivative, halves, stiff_diag = float_tables()
    part_count = lax.axis_size("parts")
    own_index = lax.axis_index("parts")
    elem_count = rhs.shape[1]
    record_count = rec_elem.shape[0]
    capacity = send_rec.shape[0] // part_count
    far_reach = 2 * LD - 1
    rec_col = rec_dir * elem_count + rec_elem
    code_float = elem_code.astype(jnp.float32)
    elem_size = 0.5 * code_float
    inv_size = jnp.where(elem_code > 0, 2.0 / jnp.maximum(code_float, 1.0), 0.0)
    live_elem = elem_code > 0
    own_size = elem_size[rec_elem]
    mortar_size = jnp.where(rec_sub < 4, 0.5 * own_size, own_size)
    live_rec = (rec_sub < 5).astype(jnp.float32)
    is_bound = rec_peer < 0
    is_local = rec_peer == own_index
    is_remote = jnp.logical_and(jnp.logical_not(is_bound), jnp.logical_not(is_local))
    offset = own_index - rec_peer
    position = jnp.where(offset < 0, offset + far_reach, offset + far_reach - 1)
    remote_col = jnp.where(is_remote, position * capacity + rec_index, 0)
    pool_col = jnp.where(is_local, rec_index, record_count + remote_col)
    step_list = list(range(-far_reach, 0)) + list(range(1, far_reach + 1))
    step_offsets = jnp.asarray(np.array(step_list, dtype=np.int32))
    targets = jnp.clip(own_index + step_offsets, 0, part_count - 1)
    send_cols = send_rec.reshape(part_count, capacity)[targets].reshape(-1)
    weight_cube = weights[:, None, None] * weights[None, :, None] * weights[None, None, :]
    face_weight = (weights[:, None] * weights[None, :]).reshape(36)
    precond_scale = inv_size[None, :] / stiff_diag[:, None]

    def send_traces(own_traces):
        outgoing_all = own_traces[:, send_cols]
        blocks = []
        for index_pos in range(2 * far_reach):
            blocks.append(
                shifted(
                    outgoing_all[:, index_pos * capacity : (index_pos + 1) * capacity],
                    "parts",
                    step_list[index_pos],
                )
            )
        return jnp.concatenate(blocks, axis=1)

    def apply_operator(flat_field):
        nodal_field = flat_field.reshape(6, 6, 6, elem_count)
        face_value, face_slope = face_traces(nodal_field, inv_size, derivative)
        face_both = jnp.concatenate([face_value, face_slope], axis=0)
        picked = face_both[:, rec_col].reshape(2, 6, 6, record_count)
        own_traces = onto_both(picked, rec_sub, halves).reshape(72, record_count)
        received = send_traces(own_traces)
        volume = volume_term(nodal_field, elem_size, weight_cube, derivative)
        pool = jnp.concatenate([own_traces, received], axis=1)
        partner = pool[:, pool_col]
        term_value, term_slope = mortar_terms(
            own_traces, partner, is_bound, mortar_size, live_rec, face_weight
        )
        terms = jnp.concatenate([term_value, term_slope], axis=0).reshape(2, 6, 6, record_count)
        back = off_both(terms, rec_sub, halves).reshape(72, record_count)
        face_res = jnp.zeros((72, 6 * elem_count), jnp.float32).at[:, rec_col].add(back)
        lifted = lift_faces(face_res[:36], face_res[36:], inv_size, derivative, elem_count)
        return (volume + lifted).reshape(216, elem_count)

    scale_total = 216.0 * elem_count * part_count

    def residual_of(solution):
        return jnp.where(live_elem[None, :], rhs - apply_operator(solution), 0.0)

    def record_norms(residual, precond, partials):
        local_sums = jnp.stack([jnp.sum(residual * residual), jnp.sum(residual * precond)])
        return partials + [local_sums]

    top_value = spectrum_top[0]
    bottom = top_value / BOTTOM_RATIO
    center = 0.5 * (top_value + bottom)
    radius = 0.5 * (top_value - bottom)
    sigma_ratio = center / radius
    rho_prev = 1.0 / sigma_ratio
    solution = start
    residual = residual_of(solution)
    precond = precond_scale * residual
    direction = precond / center
    partials = record_norms(residual, precond, [])
    for step_index in range(1, ITERS):
        solution = solution + direction
        residual = residual_of(solution)
        precond = precond_scale * residual
        partials = record_norms(residual, precond, partials)
        rho_next = 1.0 / (2.0 * sigma_ratio - rho_prev)
        direction = rho_next * rho_prev * direction + 2.0 * rho_next / radius * precond
        rho_prev = rho_next
    solution = solution + direction
    norms = 0.5 * jnp.log(lax.psum(jnp.stack(partials), "parts") / scale_total)
    return (solution, norms)


def solution(mesh):
    placed = (
        P(None, "parts"),
        P(None, "parts"),
        P(),
        P("parts"),
        P("parts"),
        P("parts"),
        P("parts"),
        P("parts"),
        P("parts"),
        P("parts"),
    )
    return jax.shard_map(
        on_device, mesh=mesh, in_specs=placed, out_specs=(P(None, "parts"), P()), check_vma=False
    )
```

profile of v0, /device:TPU:0, one launch (start us, length us, event | category | flops | bytes accessed | tf_op | source)
XLA Modules:
  0.0 585.8 jit_solution(8217736305569801026)
XLA Ops:
  14.2 2.4 pad_maximum_fusion
  16.5 11.0 %gather_fusion.1 = f32[3072,72]{1,0:T(8,128)} fusion(f32[72,3072]{0,1:T(8,128)S(1)} %pad_maximum_fusion, s32[3072]{0:T(1024)S(1)} %get-tuple-element.245), kind=kCustom, calls=%fused_computation.1 | custom fusion | bytes 1781760 | tf_op jit(solution)/shard_map/gather | solution.py:229
  31.8 2.2 fusion.11
  42.4 7.3 %gather_fusion.3 = f32[3584,72]{1,0:T(8,128)} fusion(f32[72,3072]{0,1:T(8,128)S(1)} %copy.568, s32[4096]{0:T(1024)S(1)} %pad_clamp_fusion), kind=kCustom, calls=%fused_computation.3 | custom fusion | bytes 2078720 | tf_op jit(solution)/shard_map/gather | solution.py:213
  49.7 2.7 fusion.150
  65.2 19.5 %gather_fusion = f32[3072]{0:T(1024)S(1)} fusion(f32[512]{0:T(512)S(1)} %get-tuple-element.399, s32[3072]{0:T(1024)S(1)} %get-tuple-element.362), kind=kCustom, calls=%fused_computation | custom fusion | bytes 36864 | tf_op jit(solution)/shard_map/gather | solution.py:194
  91.5 2.4 copy.570
  95.8 2.2 copy.565
  104.6 3.0 collective-permute-start.7
  108.6 5.5 collective-permute-start.8
  115.0 6.3 %collective-permute-start.9 = (f32[72,256]{0,1:T(8,128)}, f32[72,256]{0,1:T(8,128)S(1)}, u32[]{:S(2)}, u32[]{:S(2)}) collective-permute-start(f32[72,256]{0,1:T(8,128)} %get-tuple-element.281), channel_id=1, source_target_pairs={{0,3},{1,4},{2,5},{3,6},{4,7},{5,8},{6,9},{7,10},{8,11},{9,12},{10... | collective-permute-start | bytes 221192 | tf_op jit(solution)/shard_map/ppermute | solution.py:21
  122.3 6.1 %collective-permute-start.10 = (f32[72,256]{0,1:T(8,128)}, f32[72,256]{0,1:T(8,128)S(1)}, u32[]{:S(2)}, u32[]{:S(2)}) collective-permute-start(f32[72,256]{0,1:T(8,128)} %get-tuple-element.280), channel_id=1, source_target_pairs={{0,4},{1,5},{2,6},{3,7},{4,8},{5,9},{6,10},{7,11},{8,12},{9,13},{1... | collective-permute-start | bytes 221192 | tf_op jit(solution)/shard_map/ppermute | solution.py:21
  128.4 2.7 collective-permute-start.11
  131.2 6.8 %collective-permute-start.12 = (f32[72,256]{0,1:T(8,128)S(1)}, f32[72,256]{0,1:T(8,128)S(1)}, u32[]{:S(2)}, u32[]{:S(2)}) collective-permute-start(f32[72,256]{0,1:T(8,128)S(1)} %copy-done.60), channel_id=1, source_target_pairs={{0,6},{1,7},{2,8},{3,9},{4,10},{5,11},{6,12},{7,13},{8,14},{9,15},... | collective-permute-start | bytes 221192 | tf_op jit(solution)/shard_map/ppermute | solution.py:21
  138.1 6.8 %collective-permute-start.13 = (f32[72,256]{0,1:T(8,128)S(1)}, f32[72,256]{0,1:T(8,128)S(1)}, u32[]{:S(2)}, u32[]{:S(2)}) collective-permute-start(f32[72,256]{0,1:T(8,128)S(1)} %copy-done.59), channel_id=1, source_target_pairs={{0,7},{1,8},{2,9},{3,10},{4,11},{5,12},{6,13},{7,14},{8,15},{9,16}... | collective-permute-start | bytes 221192 | tf_op jit(solution)/shard_map/ppermute | solution.py:21
  145.1 2.2 collective-permute-done.13
  147.3 10.8 %gather_fusion.4 = f32[3072,72]{1,0:T(8,128)} fusion(f32[72,6656]{0,1:T(8,128)S(1)} %constant_dynamic-update-slice_fusion.12, s32[3072]{0:T(1024)S(1)} %get-tuple-element.243), kind=kCustom, calls=%fused_computation.4 | custom fusion | bytes 1781760 | tf_op jit(solution)/shard_map/gather | solution.py:234
  169.3 17.6 %scatter_custom_fusion = f32[72,3072]{0,1:T(8,128)S(1)} fusion(s32[3072]{0:T(1024)} %get-tuple-element.246, f32[3072,72]{1,0:T(8,128)} %copy.579, f32[]{:T(128)} %constant.511.clone.1), kind=kCustom, calls=%fused_computation.100 | custom fusion | flops 221184 | bytes 885248 | tf_op jit(solution)/shard_map/scatter-add | solution.py:240
  212.8 2.4 pad_maximum_fusion.1
  215.2 11.3 %gather_fusion.5 = f32[3072,72]{1,0:T(8,128)} fusion(f32[72,3072]{0,1:T(8,128)S(1)} %pad_maximum_fusion.1, s32[3072]{0:T(1024)S(1)} %copy-done.57), kind=kCustom, calls=%fused_computation.5 | custom fusion | bytes 1781760 | tf_op jit(solution)/shard_map/gather | solution.py:229
  230.1 2.2 fusion.7
  240.2 7.4 %gather_fusion.6 = f32[3584,72]{1,0:T(8,128)} fusion(f32[72,3072]{0,1:T(8,128)S(1)} %copy.629, s32[4096]{0:T(1024)S(1)} %pad_clamp_fusion), kind=kCustom, calls=%fused_computation.6 | custom fusion | bytes 2078720 | tf_op jit(solution)/shard_map/gather | solution.py:213
  273.0 3.0 collective-permute-start.21
  277.0 4.8 collective-permute-start.22
  282.7 6.0 %collective-permute-start.23 = (f32[72,256]{0,1:T(8,128)}, f32[72,256]{0,1:T(8,128)S(1)}, u32[]{:S(2)}, u32[]{:S(2)}) collective-permute-start(f32[72,256]{0,1:T(8,128)} %get-tuple-element.267), channel_id=1, source_target_pairs={{0,3},{1,4},{2,5},{3,6},{4,7},{5,8},{6,9},{7,10},{8,11},{9,12},{10... | collective-permute-start | bytes 221192 | tf_op jit(solution)/shard_map/ppermute | solution.py:21
  289.7 6.5 %collective-permute-start.24 = (f32[72,256]{0,1:T(8,128)}, f32[72,256]{0,1:T(8,128)S(1)}, u32[]{:S(2)}, u32[]{:S(2)}) collective-permute-start(f32[72,256]{0,1:T(8,128)} %get-tuple-element.266), channel_id=1, source_target_pairs={{0,4},{1,5},{2,6},{3,7},{4,8},{5,9},{6,10},{7,11},{8,12},{9,13},{1... | collective-permute-start | bytes 221192 | tf_op jit(solution)/shard_map/ppermute | solution.py:21
  296.2 2.9 collective-permute-start.25
  299.2 6.2 %collective-permute-start.26 = (f32[72,256]{0,1:T(8,128)S(1)}, f32[72,256]{0,1:T(8,128)S(1)}, u32[]{:S(2)}, u32[]{:S(2)}) collective-permute-start(f32[72,256]{0,1:T(8,128)S(1)} %copy-done.66), channel_id=1, source_target_pairs={{0,6},{1,7},{2,8},{3,9},{4,10},{5,11},{6,12},{7,13},{8,14},{9,15},... | collective-permute-start | bytes 221192 | tf_op jit(solution)/shard_map/ppermute | solution.py:21
  305.4 7.5 %collective-permute-start.27 = (f32[72,256]{0,1:T(8,128)S(1)}, f32[72,256]{0,1:T(8,128)S(1)}, u32[]{:S(2)}, u32[]{:S(2)}) collective-permute-start(f32[72,256]{0,1:T(8,128)S(1)} %copy-done.64), channel_id=1, source_target_pairs={{0,7},{1,8},{2,9},{3,10},{4,11},{5,12},{6,13},{7,14},{8,15},{9,16}... | collective-permute-start | bytes 221192 | tf_op jit(solution)/shard_map/ppermute | solution.py:21
  313.0 2.4 collective-permute-done.27
  315.4 10.8 %gather_fusion.7 = f32[3072,72]{1,0:T(8,128)} fusion(f32[72,6656]{0,1:T(8,128)S(1)} %constant_dynamic-update-slice_fusion.39, s32[3072]{0:T(1024)S(1)} %copy-done.49), kind=kCustom, calls=%fused_computation.7 | custom fusion | bytes 1781760 | tf_op jit(solution)/shard_map/gather | solution.py:234
  337.4 17.6 %scatter_custom_fusion.1 = f32[72,3072]{0,1:T(8,128)S(1)} fusion(s32[3072]{0:T(1024)} %get-tuple-element.246, f32[3072,72]{1,0:T(8,128)} %copy.640, f32[]{:T(128)} %constant.511.clone.1), kind=kCustom, calls=%fused_computation.98 | custom fusion | flops 221184 | bytes 885248 | tf_op jit(solution)/shard_map/scatter-add | solution.py:240
  382.9 2.4 pad_maximum_fusion.2
  385.3 11.0 %gather_fusion.8 = f32[3072,72]{1,0:T(8,128)} fusion(f32[72,3072]{0,1:T(8,128)S(1)} %pad_maximum_fusion.2, s32[3072]{0:T(1024)S(1)} %copy-done.58), kind=kCustom, calls=%fused_computation.8 | custom fusion | bytes 1781760 | tf_op jit(solution)/shard_map/gather | solution.py:229
  399.9 2.2 fusion.3
  410.0 7.4 %gather_fusion.9 = f32[3584,72]{1,0:T(8,128)} fusion(f32[72,3072]{0,1:T(8,128)S(1)} %copy.690, s32[4096]{0:T(1024)S(1)} %pad_clamp_fusion), kind=kCustom, calls=%fused_computation.9 | custom fusion | bytes 2078720 | tf_op jit(solution)/shard_map/gather | solution.py:213
  436.2 2.5 maximum_bitcast_fusion
  443.1 3.0 collective-permute-start.35
  447.1 4.8 collective-permute-start.36
  452.8 6.0 %collective-permute-start.37 = (f32[72,256]{0,1:T(8,128)S(1)}, f32[72,256]{0,1:T(8,128)S(1)}, u32[]{:S(2)}, u32[]{:S(2)}) collective-permute-start(f32[72,256]{0,1:T(8,128)S(1)} %copy-done.69), channel_id=1, source_target_pairs={{0,3},{1,4},{2,5},{3,6},{4,7},{5,8},{6,9},{7,10},{8,11},{9,12},{10... | collective-permute-start | bytes 221192 | tf_op jit(solution)/shard_map/ppermute | solution.py:21
  459.8 6.5 %collective-permute-start.38 = (f32[72,256]{0,1:T(8,128)S(1)}, f32[72,256]{0,1:T(8,128)S(1)}, u32[]{:S(2)}, u32[]{:S(2)}) collective-permute-start(f32[72,256]{0,1:T(8,128)S(1)} %copy-done.67), channel_id=1, source_target_pairs={{0,4},{1,5},{2,6},{3,7},{4,8},{5,9},{6,10},{7,11},{8,12},{9,13},{1... | collective-permute-start | bytes 221192 | tf_op jit(solution)/shard_map/ppermute | solution.py:21
  466.4 2.9 collective-permute-start.39
  469.3 6.2 %collective-permute-start.40 = (f32[72,256]{0,1:T(8,128)S(1)}, f32[72,256]{0,1:T(8,128)S(1)}, u32[]{:S(2)}, u32[]{:S(2)}) collective-permute-start(f32[72,256]{0,1:T(8,128)S(1)} %copy-done.63), channel_id=1, source_target_pairs={{0,6},{1,7},{2,8},{3,9},{4,10},{5,11},{6,12},{7,13},{8,14},{9,15},... | collective-permute-start | bytes 221192 | tf_op jit(solution)/shard_map/ppermute | solution.py:21
  475.6 7.5 %collective-permute-start.41 = (f32[72,256]{0,1:T(8,128)S(1)}, f32[72,256]{0,1:T(8,128)S(1)}, u32[]{:S(2)}, u32[]{:S(2)}) collective-permute-start(f32[72,256]{0,1:T(8,128)S(1)} %copy-done.62), channel_id=1, source_target_pairs={{0,7},{1,8},{2,9},{3,10},{4,11},{5,12},{6,13},{7,14},{8,15},{9,16}... | collective-permute-start | bytes 221192 | tf_op jit(solution)/shard_map/ppermute | solution.py:21
  483.2 2.4 collective-permute-done.41
  485.6 11.0 %gather_fusion.10 = f32[3072,72]{1,0:T(8,128)} fusion(f32[72,6656]{0,1:T(8,128)S(1)} %constant_dynamic-update-slice_fusion.66, s32[3072]{0:T(1024)S(1)} %copy-done.49), kind=kCustom, calls=%fused_computation.10 | custom fusion | bytes 1781760 | tf_op jit(solution)/shard_map/gather | solution.py:234
  507.7 17.6 %scatter_custom_fusion.2 = f32[72,3072]{0,1:T(8,128)S(1)} fusion(s32[3072]{0:T(1024)} %get-tuple-element.246, f32[3072,72]{1,0:T(8,128)} %copy.701, f32[]{:T(128)} %constant.511.clone.1), kind=kCustom, calls=%fused_computation.96 | custom fusion | flops 221184 | bytes 885248 | tf_op jit(solution)/shard_map/scatter-add | solution.py:240
  542.2 41.4 %psum.7 = f32[3,2]{1,0:T(4,128)S(1)} all-reduce(f32[3,2]{1,0:T(4,128)S(1)} %pad_maximum_fusion.6), channel_id=1, replica_groups=mesh['parts'=32] {'parts'}, use_global_device_ids=true, to_apply=%region_9.10 | all-reduce | flops 6 | bytes 48 | tf_op jit(solution)/shard_map/psum | solution.py:273
  (704 shorter events, 236.2 us)
Async XLA Ops:
  30.2 129.9 %copy-start.44 = (f32[3072]{0:T(1024)}, f32[3072]{0:T(1024)S(1)}, u32[]{:S(2)}) copy-start(f32[3072]{0:T(1024)S(1)} %get-tuple-element.359) | copy-start | bytes 36868
  52.4 47.6 %collective-permute-start = (f32[72,256]{0,1:T(8,128)}, f32[72,256]{0,1:T(8,128)}, u32[]{:S(2)}, u32[]{:S(2)}) collective-permute-start(f32[72,256]{0,1:T(8,128)} %get-tuple-element.290), channel_id=1, source_target_pairs={{7,0},{8,1},{9,2},{10,3},{11,4},{12,5},{13,6},{14,7},{15,8},{16,9}... | collective-permute-start | bytes 221192 | tf_op jit(solution)/shard_map/ppermute | solution.py:21
  53.7 48.6 %collective-permute-start.1 = (f32[72,256]{0,1:T(8,128)}, f32[72,256]{0,1:T(8,128)}, u32[]{:S(2)}, u32[]{:S(2)}) collective-permute-start(f32[72,256]{0,1:T(8,128)} %get-tuple-element.289), channel_id=1, source_target_pairs={{6,0},{7,1},{8,2},{9,3},{10,4},{11,5},{12,6},{13,7},{14,8},{15,9},... | collective-permute-start | bytes 221192 | tf_op jit(solution)/shard_map/ppermute | solution.py:21
  55.0 49.6 %collective-permute-start.2 = (f32[72,256]{0,1:T(8,128)}, f32[72,256]{0,1:T(8,128)}, u32[]{:S(2)}, u32[]{:S(2)}) collective-permute-start(f32[72,256]{0,1:T(8,128)} %get-tuple-element.288), channel_id=1, source_target_pairs={{5,0},{6,1},{7,2},{8,3},{9,4},{10,5},{11,6},{12,7},{13,8},{14,9},{... | collective-permute-start | bytes 221192 | tf_op jit(solution)/shard_map/ppermute | solution.py:21
  56.3 52.2 %collective-permute-start.3 = (f32[72,256]{0,1:T(8,128)}, f32[72,256]{0,1:T(8,128)}, u32[]{:S(2)}, u32[]{:S(2)}) collective-permute-start(f32[72,256]{0,1:T(8,128)} %get-tuple-element.287), channel_id=1, source_target_pairs={{4,0},{5,1},{6,2},{7,3},{8,4},{9,5},{10,6},{11,7},{12,8},{13,9},{1... | collective-permute-start | bytes 221192 | tf_op jit(solution)/shard_map/ppermute | solution.py:21
  57.6 57.4 %collective-permute-start.4 = (f32[72,256]{0,1:T(8,128)}, f32[72,256]{0,1:T(8,128)}, u32[]{:S(2)}, u32[]{:S(2)}) collective-permute-start(f32[72,256]{0,1:T(8,128)} %get-tuple-element.286), channel_id=1, source_target_pairs={{3,0},{4,1},{5,2},{6,3},{7,4},{8,5},{9,6},{10,7},{11,8},{12,9},{13... | collective-permute-start | bytes 221192 | tf_op jit(solution)/shard_map/ppermute | solution.py:21
  84.7 75.3 %copy-start.50 = (f32[3072]{0:T(1024)}, f32[3072]{0:T(1024)S(1)}, u32[]{:S(2)}) copy-start(f32[3072]{0:T(1024)S(1)} %get-tuple-element.241) | copy-start | bytes 36868
  84.7 75.3 %copy-start.52 = (f32[3072]{0:T(1024)}, f32[3072]{0:T(1024)S(1)}, u32[]{:S(2)}) copy-start(f32[3072]{0:T(1024)S(1)} %get-tuple-element.242) | copy-start | bytes 36868
  84.8 75.3 %copy-start.54 = (f32[3072]{0:T(1024)}, f32[3072]{0:T(1024)S(1)}, u32[]{:S(2)}) copy-start(f32[3072]{0:T(1024)S(1)} %get-tuple-element.357) | copy-start | bytes 36868
  84.8 62.5 %copy-start.48 = (s32[3072]{0:T(1024)}, s32[3072]{0:T(1024)S(1)}, u32[]{:S(2)}) copy-start(s32[3072]{0:T(1024)S(1)} %get-tuple-element.243) | copy-start | bytes 36868
  85.4 74.7 %copy-start.46 = (f32[3072]{0:T(1024)}, f32[3072]{0:T(1024)S(1)}, u32[]{:S(2)}) copy-start(f32[3072]{0:T(1024)S(1)} %broadcast_select_fusion) | copy-start | bytes 36868
  100.0 22.3 %collective-permute-start.5 = (f32[72,256]{0,1:T(8,128)}, f32[72,256]{0,1:T(8,128)S(1)}, u32[]{:S(2)}, u32[]{:S(2)}) collective-permute-start(f32[72,256]{0,1:T(8,128)} %get-tuple-element.285), channel_id=1, source_target_pairs={{2,0},{3,1},{4,2},{5,3},{6,4},{7,5},{8,6},{9,7},{10,8},{11,9},{12,... | collective-permute-start | bytes 221192 | tf_op jit(solution)/shard_map/ppermute | solution.py:21
  102.4 26.0 %collective-permute-start.6 = (f32[72,256]{0,1:T(8,128)}, f32[72,256]{0,1:T(8,128)S(1)}, u32[]{:S(2)}, u32[]{:S(2)}) collective-permute-start(f32[72,256]{0,1:T(8,128)} %get-tuple-element.284), channel_id=1, source_target_pairs={{1,0},{2,1},{3,2},{4,3},{5,4},{6,5},{7,6},{8,7},{9,8},{10,9},{11,1... | collective-permute-start | bytes 221192 | tf_op jit(solution)/shard_map/ppermute | solution.py:21
  104.6 26.6 %collective-permute-start.7 = (f32[72,256]{0,1:T(8,128)}, f32[72,256]{0,1:T(8,128)S(1)}, u32[]{:S(2)}, u32[]{:S(2)}) collective-permute-start(f32[72,256]{0,1:T(8,128)} %get-tuple-element.283), channel_id=1, source_target_pairs={{0,1},{1,2},{2,3},{3,4},{4,5},{5,6},{6,7},{7,8},{8,9},{9,10},{10,1... | collective-permute-start | bytes 221192 | tf_op jit(solution)/shard_map/ppermute | solution.py:21
  108.6 29.5 %collective-permute-start.8 = (f32[72,256]{0,1:T(8,128)}, f32[72,256]{0,1:T(8,128)S(1)}, u32[]{:S(2)}, u32[]{:S(2)}) collective-permute-start(f32[72,256]{0,1:T(8,128)} %get-tuple-element.282), channel_id=1, source_target_pairs={{0,2},{1,3},{2,4},{3,5},{4,6},{5,7},{6,8},{7,9},{8,10},{9,11},{10,... | collective-permute-start | bytes 221192 | tf_op jit(solution)/shard_map/ppermute | solution.py:21
  115.0 29.9 %collective-permute-start.9 = (f32[72,256]{0,1:T(8,128)}, f32[72,256]{0,1:T(8,128)S(1)}, u32[]{:S(2)}, u32[]{:S(2)}) collective-permute-start(f32[72,256]{0,1:T(8,128)} %get-tuple-element.281), channel_id=1, source_target_pairs={{0,3},{1,4},{2,5},{3,6},{4,7},{5,8},{6,9},{7,10},{8,11},{9,12},{10... | collective-permute-start | bytes 221192 | tf_op jit(solution)/shard_map/ppermute | solution.py:21
  122.3 22.7 %collective-permute-start.10 = (f32[72,256]{0,1:T(8,128)}, f32[72,256]{0,1:T(8,128)S(1)}, u32[]{:S(2)}, u32[]{:S(2)}) collective-permute-start(f32[72,256]{0,1:T(8,128)} %get-tuple-element.280), channel_id=1, source_target_pairs={{0,4},{1,5},{2,6},{3,7},{4,8},{5,9},{6,10},{7,11},{8,12},{9,13},{1... | collective-permute-start | bytes 221192 | tf_op jit(solution)/shard_map/ppermute | solution.py:21
  128.4 16.6 %collective-permute-start.11 = (f32[72,256]{0,1:T(8,128)S(1)}, f32[72,256]{0,1:T(8,128)S(1)}, u32[]{:S(2)}, u32[]{:S(2)}) collective-permute-start(f32[72,256]{0,1:T(8,128)S(1)} %copy-done.61), channel_id=1, source_target_pairs={{0,5},{1,6},{2,7},{3,8},{4,9},{5,10},{6,11},{7,12},{8,13},{9,14},{... | collective-permute-start | bytes 221192 | tf_op jit(solution)/shard_map/ppermute | solution.py:21
  131.2 13.9 %collective-permute-start.12 = (f32[72,256]{0,1:T(8,128)S(1)}, f32[72,256]{0,1:T(8,128)S(1)}, u32[]{:S(2)}, u32[]{:S(2)}) collective-permute-start(f32[72,256]{0,1:T(8,128)S(1)} %copy-done.60), channel_id=1, source_target_pairs={{0,6},{1,7},{2,8},{3,9},{4,10},{5,11},{6,12},{7,13},{8,14},{9,15},... | collective-permute-start | bytes 221192 | tf_op jit(solution)/shard_map/ppermute | solution.py:21
  138.1 9.2 %collective-permute-start.13 = (f32[72,256]{0,1:T(8,128)S(1)}, f32[72,256]{0,1:T(8,128)S(1)}, u32[]{:S(2)}, u32[]{:S(2)}) collective-permute-start(f32[72,256]{0,1:T(8,128)S(1)} %copy-done.59), channel_id=1, source_target_pairs={{0,7},{1,8},{2,9},{3,10},{4,11},{5,12},{6,13},{7,14},{8,15},{9,16}... | collective-permute-start | bytes 221192 | tf_op jit(solution)/shard_map/ppermute | solution.py:21
  250.3 18.0 %collective-permute-start.14 = (f32[72,256]{0,1:T(8,128)}, f32[72,256]{0,1:T(8,128)}, u32[]{:S(2)}, u32[]{:S(2)}) collective-permute-start(f32[72,256]{0,1:T(8,128)} %get-tuple-element.276), channel_id=1, source_target_pairs={{7,0},{8,1},{9,2},{10,3},{11,4},{12,5},{13,6},{14,7},{15,8},{16,9}... | collective-permute-start | bytes 221192 | tf_op jit(solution)/shard_map/ppermute | solution.py:21
  259.1 11.7 %collective-permute-start.15 = (f32[72,256]{0,1:T(8,128)}, f32[72,256]{0,1:T(8,128)}, u32[]{:S(2)}, u32[]{:S(2)}) collective-permute-start(f32[72,256]{0,1:T(8,128)} %get-tuple-element.275), channel_id=1, source_target_pairs={{6,0},{7,1},{8,2},{9,3},{10,4},{11,5},{12,6},{13,7},{14,8},{15,9},... | collective-permute-start | bytes 221192 | tf_op jit(solution)/shard_map/ppermute | solution.py:21
  260.4 12.6 %collective-permute-start.16 = (f32[72,256]{0,1:T(8,128)}, f32[72,256]{0,1:T(8,128)}, u32[]{:S(2)}, u32[]{:S(2)}) collective-permute-start(f32[72,256]{0,1:T(8,128)} %get-tuple-element.274), channel_id=1, source_target_pairs={{5,0},{6,1},{7,2},{8,3},{9,4},{10,5},{11,6},{12,7},{13,8},{14,9},{... | collective-permute-start | bytes 221192 | tf_op jit(solution)/shard_map/ppermute | solution.py:21
  261.7 15.3 %collective-permute-start.17 = (f32[72,256]{0,1:T(8,128)}, f32[72,256]{0,1:T(8,128)}, u32[]{:S(2)}, u32[]{:S(2)}) collective-permute-start(f32[72,256]{0,1:T(8,128)} %get-tuple-element.273), channel_id=1, source_target_pairs={{4,0},{5,1},{6,2},{7,3},{8,4},{9,5},{10,6},{11,7},{12,8},{13,9},{1... | collective-permute-start | bytes 221192 | tf_op jit(solution)/shard_map/ppermute | solution.py:21
  263.0 19.7 %collective-permute-start.18 = (f32[72,256]{0,1:T(8,128)}, f32[72,256]{0,1:T(8,128)}, u32[]{:S(2)}, u32[]{:S(2)}) collective-permute-start(f32[72,256]{0,1:T(8,128)} %get-tuple-element.272), channel_id=1, source_target_pairs={{3,0},{4,1},{5,2},{6,3},{7,4},{8,5},{9,6},{10,7},{11,8},{12,9},{13... | collective-permute-start | bytes 221192 | tf_op jit(solution)/shard_map/ppermute | solution.py:21
  268.4 21.3 %collective-permute-start.19 = (f32[72,256]{0,1:T(8,128)}, f32[72,256]{0,1:T(8,128)S(1)}, u32[]{:S(2)}, u32[]{:S(2)}) collective-permute-start(f32[72,256]{0,1:T(8,128)} %get-tuple-element.271), channel_id=1, source_target_pairs={{2,0},{3,1},{4,2},{5,3},{6,4},{7,5},{8,6},{9,7},{10,8},{11,9},{12,... | collective-permute-start | bytes 221192 | tf_op jit(solution)/shard_map/ppermute | solution.py:21
  270.8 25.4 %collective-permute-start.20 = (f32[72,256]{0,1:T(8,128)}, f32[72,256]{0,1:T(8,128)S(1)}, u32[]{:S(2)}, u32[]{:S(2)}) collective-permute-start(f32[72,256]{0,1:T(8,128)} %get-tuple-element.270), channel_id=1, source_target_pairs={{1,0},{2,1},{3,2},{4,3},{5,4},{6,5},{7,6},{8,7},{9,8},{10,9},{11,1... | collective-permute-start | bytes 221192 | tf_op jit(solution)/shard_map/ppermute | solution.py:21
  273.0 26.2 %collective-permute-start.21 = (f32[72,256]{0,1:T(8,128)}, f32[72,256]{0,1:T(8,128)S(1)}, u32[]{:S(2)}, u32[]{:S(2)}) collective-permute-start(f32[72,256]{0,1:T(8,128)} %get-tuple-element.269), channel_id=1, source_target_pairs={{0,1},{1,2},{2,3},{3,4},{4,5},{5,6},{6,7},{7,8},{8,9},{9,10},{10,1... | collective-permute-start | bytes 221192 | tf_op jit(solution)/shard_map/ppermute | solution.py:21
  277.0 28.4 %collective-permute-start.22 = (f32[72,256]{0,1:T(8,128)}, f32[72,256]{0,1:T(8,128)S(1)}, u32[]{:S(2)}, u32[]{:S(2)}) collective-permute-start(f32[72,256]{0,1:T(8,128)} %get-tuple-element.268), channel_id=1, source_target_pairs={{0,2},{1,3},{2,4},{3,5},{4,6},{5,7},{6,8},{7,9},{8,10},{9,11},{10,... | collective-permute-start | bytes 221192 | tf_op jit(solution)/shard_map/ppermute | solution.py:21
  282.7 30.2 %collective-permute-start.23 = (f32[72,256]{0,1:T(8,128)}, f32[72,256]{0,1:T(8,128)S(1)}, u32[]{:S(2)}, u32[]{:S(2)}) collective-permute-start(f32[72,256]{0,1:T(8,128)} %get-tuple-element.267), channel_id=1, source_target_pairs={{0,3},{1,4},{2,5},{3,6},{4,7},{5,8},{6,9},{7,10},{8,11},{9,12},{10... | collective-permute-start | bytes 221192 | tf_op jit(solution)/shard_map/ppermute | solution.py:21
  289.7 23.3 %collective-permute-start.24 = (f32[72,256]{0,1:T(8,128)}, f32[72,256]{0,1:T(8,128)S(1)}, u32[]{:S(2)}, u32[]{:S(2)}) collective-permute-start(f32[72,256]{0,1:T(8,128)} %get-tuple-element.266), channel_id=1, source_target_pairs={{0,4},{1,5},{2,6},{3,7},{4,8},{5,9},{6,10},{7,11},{8,12},{9,13},{1... | collective-permute-start | bytes 221192 | tf_op jit(solution)/shard_map/ppermute | solution.py:21
  296.2 16.8 %collective-permute-start.25 = (f32[72,256]{0,1:T(8,128)S(1)}, f32[72,256]{0,1:T(8,128)S(1)}, u32[]{:S(2)}, u32[]{:S(2)}) collective-permute-start(f32[72,256]{0,1:T(8,128)S(1)} %copy-done.68), channel_id=1, source_target_pairs={{0,5},{1,6},{2,7},{3,8},{4,9},{5,10},{6,11},{7,12},{8,13},{9,14},{... | collective-permute-start | bytes 221192 | tf_op jit(solution)/shard_map/ppermute | solution.py:21
  299.2 13.8 %collective-permute-start.26 = (f32[72,256]{0,1:T(8,128)S(1)}, f32[72,256]{0,1:T(8,128)S(1)}, u32[]{:S(2)}, u32[]{:S(2)}) collective-permute-start(f32[72,256]{0,1:T(8,128)S(1)} %copy-done.66), channel_id=1, source_target_pairs={{0,6},{1,7},{2,8},{3,9},{4,10},{5,11},{6,12},{7,13},{8,14},{9,15},... | collective-permute-start | bytes 221192 | tf_op jit(solution)/shard_map/ppermute | solution.py:21
  305.4 10.0 %collective-permute-start.27 = (f32[72,256]{0,1:T(8,128)S(1)}, f32[72,256]{0,1:T(8,128)S(1)}, u32[]{:S(2)}, u32[]{:S(2)}) collective-permute-start(f32[72,256]{0,1:T(8,128)S(1)} %copy-done.64), channel_id=1, source_target_pairs={{0,7},{1,8},{2,9},{3,10},{4,11},{5,12},{6,13},{7,14},{8,15},{9,16}... | collective-permute-start | bytes 221192 | tf_op jit(solution)/shard_map/ppermute | solution.py:21
  423.0 15.7 %collective-permute-start.28 = (f32[72,256]{0,1:T(8,128)}, f32[72,256]{0,1:T(8,128)}, u32[]{:S(2)}, u32[]{:S(2)}) collective-permute-start(f32[72,256]{0,1:T(8,128)} %get-tuple-element.262), channel_id=1, source_target_pairs={{7,0},{8,1},{9,2},{10,3},{11,4},{12,5},{13,6},{14,7},{15,8},{16,9}... | collective-permute-start | bytes 221192 | tf_op jit(solution)/shard_map/ppermute | solution.py:21
  424.3 16.6 %collective-permute-start.29 = (f32[72,256]{0,1:T(8,128)}, f32[72,256]{0,1:T(8,128)}, u32[]{:S(2)}, u32[]{:S(2)}) collective-permute-start(f32[72,256]{0,1:T(8,128)} %get-tuple-element.261), channel_id=1, source_target_pairs={{6,0},{7,1},{8,2},{9,3},{10,4},{11,5},{12,6},{13,7},{14,8},{15,9},... | collective-permute-start | bytes 221192 | tf_op jit(solution)/shard_map/ppermute | solution.py:21
  425.6 17.5 %collective-permute-start.30 = (f32[72,256]{0,1:T(8,128)}, f32[72,256]{0,1:T(8,128)}, u32[]{:S(2)}, u32[]{:S(2)}) collective-permute-start(f32[72,256]{0,1:T(8,128)} %get-tuple-element.260), channel_id=1, source_target_pairs={{5,0},{6,1},{7,2},{8,3},{9,4},{10,5},{11,6},{12,7},{13,8},{14,9},{... | collective-permute-start | bytes 221192 | tf_op jit(solution)/shard_map/ppermute | solution.py:21
  426.9 20.2 %collective-permute-start.31 = (f32[72,256]{0,1:T(8,128)}, f32[72,256]{0,1:T(8,128)}, u32[]{:S(2)}, u32[]{:S(2)}) collective-permute-start(f32[72,256]{0,1:T(8,128)} %get-tuple-element.259), channel_id=1, source_target_pairs={{4,0},{5,1},{6,2},{7,3},{8,4},{9,5},{10,6},{11,7},{12,8},{13,9},{1... | collective-permute-start | bytes 221192 | tf_op jit(solution)/shard_map/ppermute | solution.py:21
  428.2 24.7 %collective-permute-start.32 = (f32[72,256]{0,1:T(8,128)}, f32[72,256]{0,1:T(8,128)}, u32[]{:S(2)}, u32[]{:S(2)}) collective-permute-start(f32[72,256]{0,1:T(8,128)} %get-tuple-element.258), channel_id=1, source_target_pairs={{3,0},{4,1},{5,2},{6,3},{7,4},{8,5},{9,6},{10,7},{11,8},{12,9},{13... | collective-permute-start | bytes 221192 | tf_op jit(solution)/shard_map/ppermute | solution.py:21
  438.6 21.2 %collective-permute-start.33 = (f32[72,256]{0,1:T(8,128)S(1)}, f32[72,256]{0,1:T(8,128)S(1)}, u32[]{:S(2)}, u32[]{:S(2)}) collective-permute-start(f32[72,256]{0,1:T(8,128)S(1)} %copy-done.73), channel_id=1, source_target_pairs={{2,0},{3,1},{4,2},{5,3},{6,4},{7,5},{8,6},{9,7},{10,8},{11,9},{12,... | collective-permute-start | bytes 221192 | tf_op jit(solution)/shard_map/ppermute | solution.py:21
  440.9 25.5 %collective-permute-start.34 = (f32[72,256]{0,1:T(8,128)S(1)}, f32[72,256]{0,1:T(8,128)S(1)}, u32[]{:S(2)}, u32[]{:S(2)}) collective-permute-start(f32[72,256]{0,1:T(8,128)S(1)} %copy-done.72), channel_id=1, source_target_pairs={{1,0},{2,1},{3,2},{4,3},{5,4},{6,5},{7,6},{8,7},{9,8},{10,9},{11,1... | collective-permute-start | bytes 221192 | tf_op jit(solution)/shard_map/ppermute | solution.py:21
  443.1 26.2 %collective-permute-start.35 = (f32[72,256]{0,1:T(8,128)S(1)}, f32[72,256]{0,1:T(8,128)S(1)}, u32[]{:S(2)}, u32[]{:S(2)}) collective-permute-start(f32[72,256]{0,1:T(8,128)S(1)} %copy-done.71), channel_id=1, source_target_pairs={{0,1},{1,2},{2,3},{3,4},{4,5},{5,6},{6,7},{7,8},{8,9},{9,10},{10,1... | collective-permute-start | bytes 221192 | tf_op jit(solution)/shard_map/ppermute | solution.py:21
  447.1 28.5 %collective-permute-start.36 = (f32[72,256]{0,1:T(8,128)S(1)}, f32[72,256]{0,1:T(8,128)S(1)}, u32[]{:S(2)}, u32[]{:S(2)}) collective-permute-start(f32[72,256]{0,1:T(8,128)S(1)} %copy-done.70), channel_id=1, source_target_pairs={{0,2},{1,3},{2,4},{3,5},{4,6},{5,7},{6,8},{7,9},{8,10},{9,11},{10,... | collective-permute-start | bytes 221192 | tf_op jit(solution)/shard_map/ppermute | solution.py:21
  452.8 30.2 %collective-permute-start.37 = (f32[72,256]{0,1:T(8,128)S(1)}, f32[72,256]{0,1:T(8,128)S(1)}, u32[]{:S(2)}, u32[]{:S(2)}) collective-permute-start(f32[72,256]{0,1:T(8,128)S(1)} %copy-done.69), channel_id=1, source_target_pairs={{0,3},{1,4},{2,5},{3,6},{4,7},{5,8},{6,9},{7,10},{8,11},{9,12},{10... | collective-permute-start | bytes 221192 | tf_op jit(solution)/shard_map/ppermute | solution.py:21
  459.8 23.3 %collective-permute-start.38 = (f32[72,256]{0,1:T(8,128)S(1)}, f32[72,256]{0,1:T(8,128)S(1)}, u32[]{:S(2)}, u32[]{:S(2)}) collective-permute-start(f32[72,256]{0,1:T(8,128)S(1)} %copy-done.67), channel_id=1, source_target_pairs={{0,4},{1,5},{2,6},{3,7},{4,8},{5,9},{6,10},{7,11},{8,12},{9,13},{1... | collective-permute-start | bytes 221192 | tf_op jit(solution)/shard_map/ppermute | solution.py:21
  466.4 16.8 %collective-permute-start.39 = (f32[72,256]{0,1:T(8,128)S(1)}, f32[72,256]{0,1:T(8,128)S(1)}, u32[]{:S(2)}, u32[]{:S(2)}) collective-permute-start(f32[72,256]{0,1:T(8,128)S(1)} %copy-done.65), channel_id=1, source_target_pairs={{0,5},{1,6},{2,7},{3,8},{4,9},{5,10},{6,11},{7,12},{8,13},{9,14},{... | collective-permute-start | bytes 221192 | tf_op jit(solution)/shard_map/ppermute | solution.py:21
  469.3 13.8 %collective-permute-start.40 = (f32[72,256]{0,1:T(8,128)S(1)}, f32[72,256]{0,1:T(8,128)S(1)}, u32[]{:S(2)}, u32[]{:S(2)}) collective-permute-start(f32[72,256]{0,1:T(8,128)S(1)} %copy-done.63), channel_id=1, source_target_pairs={{0,6},{1,7},{2,8},{3,9},{4,10},{5,11},{6,12},{7,13},{8,14},{9,15},... | collective-permute-start | bytes 221192 | tf_op jit(solution)/shard_map/ppermute | solution.py:21
  475.6 10.0 %collective-permute-start.41 = (f32[72,256]{0,1:T(8,128)S(1)}, f32[72,256]{0,1:T(8,128)S(1)}, u32[]{:S(2)}, u32[]{:S(2)}) collective-permute-start(f32[72,256]{0,1:T(8,128)S(1)} %copy-done.62), channel_id=1, source_target_pairs={{0,7},{1,8},{2,9},{3,10},{4,11},{5,12},{6,13},{7,14},{8,15},{9,16}... | collective-permute-start | bytes 221192 | tf_op jit(solution)/shard_map/ppermute | solution.py:21
  (108 other events, 819.8 us)
where the time goes:
time: 594 us; the launch traced here: 586 us
  local copies, waits for them, and re-layouts  227 us (38%)
  starting transfers between devices  139 us (23%)
  other arithmetic  89.5 us (15%)
  matrix products  75.6 us (13%)
  blocking collectives  41.4 us (7%)
  waiting for transfers between devices  7 us (1%)
  between operations  6.14 us (1%)
    ppermute x42, starting transfers between devices, shifted(): return lax.ppermute(shard, axis, pairs)  139 us
    scatter-add x3, other arithmetic, apply_operator(): jnp.zeros((72, 6 * elem_count), jnp.float32).at[:, rec_col].add(back)  52.9 us
    psum x1, blocking collectives, on_device(): norms = 0.5 * jnp.log(lax.psum(jnp.stack(partials), 'parts') / scale_total)  41.4 us
    unnamed x321, local copies, waits for them, and re-layouts  40 us
    gather x6, local copies, waits for them, and re-layouts, apply_operator(): picked = face_both[:, rec_col].reshape(2, 6, 6, record_count)  38.9 us
    gather x6, local copies, waits for them, and re-layouts, apply_operator(): partner = pool[:, pool_col]  38.5 us
    gather x3, local copies, waits for them, and re-layouts, send_traces(): outgoing_all = own_traces[:, send_cols]  22.1 us
    gather x1, local copies, waits for them, and re-layouts, on_device(): own_size = elem_size[rec_elem]  19.5 us
  transfers between devices with their start and end apart: 42, of which 3 were waited for; matrix products, arithmetic and copies ran while one was open for 13% of the time, Pallas kernels for 0%

commit v1 on v0

v1 whole, which is shorter than its diff:
```python
import functools
import math

import jax
import jax.numpy as jnp
import numpy as np
from jax import lax
from jax.experimental import pallas as pl
from jax.experimental.pallas import tpu as pltpu
from jax.sharding import PartitionSpec as P

LD = 4
ITERS = 3


PENALTY = 36.0
BOTTOM_RATIO = 8.0


def lobatto_tables():
    root_seven = math.sqrt(7.0)
    inner_root = math.sqrt(1.0 / 3.0 - 2.0 * root_seven / 21.0)
    outer_root = math.sqrt(1.0 / 3.0 + 2.0 * root_seven / 21.0)
    points = (np.array([-1.0, -outer_root, -inner_root, inner_root, outer_root, 1.0]) + 1.0) / 2.0
    weights = (
        np.array(
            [
                1.0 / 15.0,
                (14.0 - root_seven) / 30.0,
                (14.0 + root_seven) / 30.0,
                (14.0 + root_seven) / 30.0,
                (14.0 - root_seven) / 30.0,
                1.0 / 15.0,
            ]
        )
        / 2.0
    )
    barycentric = np.array(
        [1.0 / np.prod([points[j] - points[k] for k in range(6) if k != j]) for j in range(6)]
    )
    derivative = np.zeros((6, 6))
    for i in range(6):
        for j in range(6):
            if i != j:
                derivative[i, j] = barycentric[j] / barycentric[i] / (points[i] - points[j])
        derivative[i, i] = -np.sum(derivative[i])
    halves = np.zeros((2, 6, 6))
    for which_half in range(2):
        targets = (points + which_half) / 2.0
        for i in range(6):
            for j in range(6):
                halves[which_half, i, j] = np.prod(
                    [(targets[i] - points[k]) / (points[j] - points[k]) for k in range(6) if k != j]
                )
    column_sums = np.sum(derivative * derivative * weights[:, None], axis=0)
    stiff_diag = (
        column_sums[:, None, None] * weights[None, :, None] * weights[None, None, :]
        + weights[:, None, None] * column_sums[None, :, None] * weights[None, None, :]
        + weights[:, None, None] * weights[None, :, None] * column_sums[None, None, :]
    )
    return (weights, derivative, halves, stiff_diag.reshape(216))


BF16 = jnp.bfloat16
F32 = jnp.float32


def split_np(matrix):
    high = np.asarray(matrix, np.float32).astype(BF16)
    low = (np.asarray(matrix, np.float64) - high.astype(np.float64)).astype(np.float32).astype(BF16)
    return high, low


def operators():
    weights, derivative, halves, stiff_diag = lobatto_tables()
    eye = np.eye(6)
    trace_rows = []
    for direction in range(6):
        axis_index = direction // 2
        layer_index = 5 * (direction % 2)
        orientation = 2.0 * (direction % 2) - 1.0
        for row in (eye[layer_index], orientation * derivative[layer_index]):
            factors = [eye, eye, eye]
            factors[axis_index] = row[None, :]
            trace_rows.append(np.kron(np.kron(factors[0], factors[1]), factors[2]))
    traces = np.concatenate(trace_rows, axis=0)
    stiff_1d = derivative.T @ (weights[:, None] * derivative)
    mass = np.diag(weights)
    stiffness = (
        np.kron(np.kron(stiff_1d, mass), mass)
        + np.kron(np.kron(mass, stiff_1d), mass)
        + np.kron(np.kron(mass, mass), stiff_1d)
    )
    blocks = []
    for sub in range(4):
        quarter = np.kron(halves[sub % 2], halves[sub // 2])
        blocks.append(np.kron(np.eye(2), quarter))
    return traces, stiffness, np.concatenate(blocks, axis=0), np.outer(weights, weights).reshape(36, 1), stiff_diag


def split(value):
    high = value.astype(BF16)
    return high, (value - high.astype(F32)).astype(BF16)


def dot(left, right):
    return jnp.dot(left, right, preferred_element_type=F32)


def dot3(left_high, left_low, right):
    high, low = split(right)
    return dot(left_high, high) + (dot(left_high, low) + dot(left_low, high))


def one_hot(index_row, rows, base=0):
    count = index_row.shape[1]
    position = lax.broadcasted_iota(jnp.int32, (rows, count), 0)
    return jnp.where(position == index_row - base, 1.0, 0.0).astype(BF16)


def pick(traces, elem, direction, sub, onto):
    wide = dot(traces, one_hot(elem, traces.shape[1]))
    face = jnp.zeros((72, elem.shape[1]), F32)
    for d in range(6):
        both = wide[72 * d : 72 * d + 72] + wide[432 + 72 * d : 432 + 72 * d + 72]
        face = jnp.where(direction == d, both, face)
    high, low = split(face)
    quarters = dot(onto, jnp.concatenate([high, low, high], axis=0))
    result = face
    for s in range(4):
        result = jnp.where(sub == s, quarters[72 * s : 72 * s + 72], result)
    return result


def send_kernel(x_ref, inv_ref, code_ref, mat_high, mat_low, onto_ref, out_ref, traces_ref):
    @pl.when(pl.program_id(0) == 0)
    def _():
        raw = dot3(mat_high[...], mat_low[...], x_ref[...])
        row = lax.broadcasted_iota(jnp.int32, raw.shape, 0)
        raw = jnp.where(lax.rem(row, 72) >= 36, raw * inv_ref[...], raw)
        high, low = split(raw)
        traces_ref[0:432] = high
        traces_ref[432:864] = low

    code = code_ref[...]
    out_ref[...] = pick(traces_ref[...], code[0:1], code[1:2], code[2:3], onto_ref[...])


def exchange_kernel(steps, axis, capacity, src_ref, dst_ref, send_sem, recv_sem):
    count = lax.axis_size(axis)
    me = lax.axis_index(axis)
    barrier = pltpu.get_barrier_semaphore()
    peers = [lax.rem(me + step + count, count) for step in steps]
    for peer in peers:
        pl.semaphore_signal(barrier, inc=1, device_id=(peer,), device_id_type=pl.DeviceIdType.MESH)
    pl.semaphore_wait(barrier, len(steps))
    copies = []
    for k, peer in enumerate(peers):
        part = pl.ds(k * capacity, capacity)
        copy = pltpu.make_async_remote_copy(
            src_ref=src_ref.at[:, part],
            dst_ref=dst_ref.at[:, part],
            send_sem=send_sem.at[k],
            recv_sem=recv_sem.at[k],
            device_id=(peer,),
            device_id_type=pl.DeviceIdType.MESH,
        )
        copy.start()
        copies.append(copy)
    for copy in copies:
        copy.wait()


def apply_kernel(
    coef_ref, x_ref, dirn_ref, rhs_ref, elem_ref, prec_ref, traces_ref, recv_ref, code_ref, rows_ref,
    size_ref, onto_ref, off_ref, weight_ref, stiff_high, stiff_low, lift_high, lift_low,
    x_out, dirn_out, sums_out, pool, total,
):
    chunk = pool.shape[2]

    @pl.when(pl.program_id(0) == 0)
    def _():
        for k in range(pool.shape[0]):
            high, low = split(recv_ref[:, k * chunk : (k + 1) * chunk])
            pool[k, 0:72] = high
            pool[k, 72:144] = low
        total[...] = jnp.zeros_like(total)

    code = code_ref[...]
    elem, direction, sub = code[0:1], code[1:2], code[2:3]
    bound = code[6:7] > 0
    width = elem.shape[1]
    own = pick(traces_ref[...], elem, direction, sub, onto_ref[...])
    near = pick(traces_ref[...], code[3:4], code[4:5], code[5:6], onto_ref[...])

    def far_step(k, carry):
        return carry + dot(pool[k], one_hot(code[7:8], chunk, k * chunk))

    far = lax.fori_loop(0, pool.shape[0], far_step, jnp.zeros((144, width), F32))
    partner = near + (far[0:72] + far[72:144])
    own_value, own_slope = own[0:36], own[36:72]
    part_value = jnp.where(bound, 0.0, partner[0:36])
    part_slope = jnp.where(bound, -own_slope, partner[36:72])
    jump = own_value - part_value
    flux = 0.5 * (own_slope - part_slope)
    mortar = size_ref[0:1]
    area = mortar * mortar
    weight = weight_ref[...] * size_ref[1:2]
    term_value = weight * (PENALTY * mortar * jump - area * flux)
    term_slope = -weight * (jnp.where(bound, 1.0, 0.5) * area) * jump
    terms = jnp.concatenate([term_value, term_slope], axis=0)
    spread = jnp.concatenate([jnp.where(sub == s, terms, 0.0) for s in range(4)], axis=0)
    spread_high, spread_low = split(spread)
    back = dot(off_ref[...], jnp.concatenate([spread_high, spread_low, spread_high], axis=0))
    back = jnp.where(sub >= 4, terms, back)
    wide = jnp.concatenate([jnp.where(direction == d, back, 0.0) for d in range(6)], axis=0)
    wide_high, wide_low = split(wide)
    lanes = lax.broadcasted_iota(jnp.int32, (width, total.shape[1]), 1)
    hot = jnp.where(lanes == rows_ref[...], 1.0, 0.0).astype(BF16)
    total[...] += dot(wide_high, hot) + dot(wide_low, hot)

    @pl.when(pl.program_id(0) == pl.num_programs(0) - 1)
    def _():
        size, inv = elem_ref[0:1], elem_ref[1:2]
        field = x_ref[...]
        row = lax.broadcasted_iota(jnp.int32, total.shape, 0)
        faces = jnp.where(lax.rem(row, 72) >= 36, total[...] * inv, total[...])
        applied = size * dot3(stiff_high[...], stiff_low[...], field)
        applied = applied + dot3(lift_high[...], lift_low[...], faces)
        residual = jnp.where(size > 0.0, rhs_ref[...] - applied, 0.0)
        scaled = residual * (inv * prec_ref[...])
        step = coef_ref[0] * dirn_ref[...] + coef_ref[1] * scaled
        dirn_out[...] = step
        x_out[...] = field + step
        sums_out[0:1] = jnp.sum(residual * residual, axis=0, keepdims=True)
        sums_out[1:2] = jnp.sum(residual * scaled, axis=0, keepdims=True)


def take_small(tables, index):
    rows = tables.shape[1] // 128
    fine = (jnp.arange(128, dtype=jnp.int32)[:, None] == (index % 128)[None, :]).astype(BF16)
    wide = jnp.dot(tables.reshape(-1, 128).astype(BF16), fine, preferred_element_type=F32)
    wide = wide.reshape(tables.shape[0], rows, -1)
    coarse = jnp.arange(rows, dtype=jnp.int32)[:, None] == (index // 128)[None, :]
    return jnp.sum(jnp.where(coarse[None], wide, 0.0), axis=1).astype(jnp.int32)


def tile(count):
    for width in (512, 256, 128):
        if count % width == 0:
            return width
    return count


def whole(shape):
    return pl.BlockSpec(shape, lambda i: (0,) * len(shape))


def on_device(
    rhs, start, spectrum_top, elem_code, rec_elem, rec_dir, rec_sub, rec_peer, rec_index, send_rec
):
    traces, stiffness, interp, face_weight, stiff_diag = operators()
    part_count = lax.axis_size("parts")
    own_index = lax.axis_index("parts")
    elem_count = rhs.shape[1]
    record_count = rec_elem.shape[0]
    capacity = send_rec.shape[0] // part_count
    far_reach = 2 * LD - 1
    code_float = elem_code.astype(F32)
    elem_size = 0.5 * code_float
    inv_size = jnp.where(elem_code > 0, 2.0 / jnp.maximum(code_float, 1.0), 0.0)
    elem_rows = jnp.stack([elem_size, inv_size])
    is_bound = rec_peer < 0
    is_local = rec_peer == own_index
    is_remote = jnp.logical_and(jnp.logical_not(is_bound), jnp.logical_not(is_local))
    offset = own_index - rec_peer
    position = jnp.where(offset < 0, offset + far_reach, offset + far_reach - 1)
    remote_col = jnp.where(is_remote, position * capacity + rec_index, -1)
    steps = list(range(-far_reach, 0)) + list(range(1, far_reach + 1))
    lists = send_rec.reshape(part_count, capacity)
    lists = jnp.concatenate([lists[part_count - far_reach :], lists, lists[:far_reach]], axis=0)
    lists = lax.dynamic_slice_in_dim(lists, own_index, 2 * far_reach + 1, 0)
    send_cols = jnp.concatenate([lists[:far_reach], lists[far_reach + 1 :]], axis=0).reshape(-1)
    send_count = send_cols.shape[0]

    own_size = 0.5 * take_small(elem_code[None], rec_elem)[0].astype(F32)
    mortar_size = jnp.where(rec_sub < 4, 0.5 * own_size, own_size)
    size_rows = jnp.stack([mortar_size, (rec_sub < 5).astype(F32)])
    tables = jnp.stack([rec_elem // 256, rec_elem % 256, rec_dir * 8 + rec_sub])
    found = take_small(tables, jnp.concatenate([send_cols, rec_index]))
    found = jnp.stack([found[0] * 256 + found[1], found[2] // 8, found[2] % 8])
    send_code = found[:, :send_count]
    near = jnp.where(is_local[None], found[:, send_count:], -1)
    rec_code = jnp.concatenate(
        [jnp.stack([rec_elem, rec_dir, rec_sub]), near, is_bound.astype(jnp.int32)[None], remote_col[None]],
        axis=0,
    )
    rec_rows = rec_elem[:, None]

    mat_high, mat_low = split_np(traces)
    lift_high, lift_low = split_np(traces.T)
    stiff_high, stiff_low = split_np(stiffness)
    onto_high, onto_low = split_np(interp)
    onto = np.concatenate([onto_high, onto_high, onto_low], axis=1)
    flat = np.concatenate([interp[72 * s : 72 * s + 72].T for s in range(4)], axis=1)
    off_high, off_low = split_np(flat)
    off = np.concatenate([off_high, off_high, off_low], axis=1)
    prec = jnp.asarray((1.0 / stiff_diag).reshape(216, 1), F32)
    weight = jnp.asarray(face_weight, F32)

    send_tile, rec_tile, chunk = tile(send_count), tile(record_count), tile(send_count)
    params = pltpu.CompilerParams(vmem_limit_bytes=60 * 1024 * 1024)
    field = (216, elem_count)

    def send_call(x):
        return pl.pallas_call(
            send_kernel,
            grid=(send_count // send_tile,),
            in_specs=[
                whole(field),
                whole((1, elem_count)),
                pl.BlockSpec((3, send_tile), lambda i: (0, i)),
                whole((432, 216)),
                whole((432, 216)),
                whole((288, 216)),
            ],
            out_specs=[pl.BlockSpec((72, send_tile), lambda i: (0, i)), whole((864, elem_count))],
            out_shape=[
                jax.ShapeDtypeStruct((72, send_count), F32),
                jax.ShapeDtypeStruct((864, elem_count), BF16),
            ],
            compiler_params=params,
            name="send_traces",
        )(x, inv_size[None], send_code, jnp.asarray(mat_high), jnp.asarray(mat_low), jnp.asarray(onto))

    def exchange(outgoing):
        return pl.pallas_call(
            functools.partial(exchange_kernel, steps, "parts", capacity),
            in_specs=[pl.BlockSpec(memory_space=pl.ANY)],
            out_specs=pl.BlockSpec(memory_space=pl.ANY),
            out_shape=jax.ShapeDtypeStruct((72, send_count), F32),
            scratch_shapes=[
                pltpu.SemaphoreType.DMA((len(steps),)),
                pltpu.SemaphoreType.DMA((len(steps),)),
            ],
            compiler_params=pltpu.CompilerParams(collective_id=0, has_side_effects=True),
            name="exchange",
        )(outgoing)

    def apply_call(coef, x, dirn, element_traces, received):
        return pl.pallas_call(
            apply_kernel,
            grid=(record_count // rec_tile,),
            in_specs=[
                pl.BlockSpec(memory_space=pltpu.SMEM),
                whole(field),
                whole(field),
                whole(field),
                whole((2, elem_count)),
                whole((216, 1)),
                whole((864, elem_count)),
                whole((72, send_count)),
                pl.BlockSpec((8, rec_tile), lambda i: (0, i)),
                pl.BlockSpec((rec_tile, 1), lambda i: (i, 0)),
                pl.BlockSpec((2, rec_tile), lambda i: (0, i)),
                whole((288, 216)),
                whole((72, 864)),
                whole((36, 1)),
                whole((216, 216)),
                whole((216, 216)),
                whole((216, 432)),
                whole((216, 432)),
            ],
            out_specs=[whole(field), whole(field), whole((2, elem_count))],
            out_shape=[
                jax.ShapeDtypeStruct(field, F32),
                jax.ShapeDtypeStruct(field, F32),
                jax.ShapeDtypeStruct((2, elem_count), F32),
            ],
            scratch_shapes=[
                pltpu.VMEM((send_count // chunk, 144, chunk), BF16),
                pltpu.VMEM((432, elem_count), F32),
            ],
            compiler_params=params,
            name="apply_operator",
        )(
            coef, x, dirn, rhs, elem_rows, prec, element_traces, received, rec_code, rec_rows, size_rows,
            jnp.asarray(onto), jnp.asarray(off), weight,
            jnp.asarray(stiff_high), jnp.asarray(stiff_low), jnp.asarray(lift_high), jnp.asarray(lift_low),
        )

    scale_total = 216.0 * elem_count * part_count
    top_value = spectrum_top[0]
    bottom = top_value / BOTTOM_RATIO
    center = 0.5 * (top_value + bottom)
    radius = 0.5 * (top_value - bottom)
    sigma_ratio = center / radius
    rho_prev = 1.0 / sigma_ratio
    coef = jnp.stack([jnp.zeros_like(center), 1.0 / center])
    x, dirn, partials = start, start, []
    for step_index in range(ITERS):
        if step_index:
            rho_next = 1.0 / (2.0 * sigma_ratio - rho_prev)
            coef = jnp.stack([rho_next * rho_prev, 2.0 * rho_next / radius])
            rho_prev = rho_next
        outgoing, element_traces = send_call(x)
        received = exchange(outgoing)
        x, dirn, sums = apply_call(coef, x, dirn, element_traces, received)
        partials.append(jnp.sum(sums, axis=1))
    norms = 0.5 * jnp.log(lax.psum(jnp.stack(partials), "parts") / scale_total)
    return (x, norms)


def solution(mesh):
    placed = (
        P(None, "parts"),
        P(None, "parts"),
        P(),
        P("parts"),
        P("parts"),
        P("parts"),
        P("parts"),
        P("parts"),
        P("parts"),
        P("parts"),
    )
    return jax.shard_map(
        on_device, mesh=mesh, in_specs=placed, out_specs=(P(None, "parts"), P()), check_vma=False
    )
```

time: 594 us -> 237 us (0.40); the launches traced: 586 us -> 236 us
  local copies, waits for them, and re-layouts: 227 us -> 5.23 us
  Pallas kernels: 0 us -> 176 us
  starting transfers between devices: 139 us -> 0 us
  other arithmetic: 89.5 us -> 11.1 us
  matrix products: 75.6 us -> 2.07 us
  waiting for transfers between devices: 7 us -> 0 us
    pallas_call x0 -> x9, Pallas kernels: none -> 176 us  [the longest x3 94.2 us: apply_call(): pl.pallas_call(apply_kernel, grid=(record_count // rec_tile,), in_specs=[...]
    ppermute x42 -> x0, starting transfers between devices: 139 us -> none  [shifted(): return lax.ppermute(shard, axis, pairs)]
    gather x17 -> x0, local copies, waits for them, and re-layouts: 120 us -> none  [the longest x6 38.9 us: apply_operator(): picked = face_both[:, rec_col].reshape(2, 6, 6, record_count)]
    dot_general x60 -> x2, matrix products: 75.6 us -> 2.07 us  [take_small(): jnp.dot(tables.reshape(-1, 128).astype(BF16), fine, preferred_element_typ...]
    scatter-add x18 -> x0, other arithmetic: 56 us -> none  [the longest x3 52.9 us: apply_operator(): jnp.zeros((72, 6 * elem_count), jnp.float32).at[:, rec_col].add(back)]
    unnamed x321 -> x10, local copies, waits for them, and re-layouts: 40 us -> 0.68 us
    slice x44 -> x5, local copies, waits for them, and re-layouts: 34.5 us -> 1.36 us  [the longest x3 0.72 us: on_device(): lists[:far_reach]]
    reshape x43 -> x1, local copies, waits for them, and re-layouts: 11.4 us -> 0.77 us  [on_device(): lists = send_rec.reshape(part_count, capacity)]
  transfers between devices with their start and end apart: 42 -> 0, of which waited for: 3 -> 0; matrix products, arithmetic and copies ran while one was open for 13% -> 0% of each run, Pallas kernels for 0% -> 0%
where the time goes in v1:
time: 237 us; the launch traced here: 236 us
  Pallas kernels  176 us (74%)
  blocking collectives  39.1 us (16%)
  other arithmetic  11.1 us (5%)
  local copies, waits for them, and re-layouts  5.23 us (2%)
    pallas_call x3, Pallas kernels, apply_call(): pl.pallas_call(apply_kernel, grid=(record_count // rec_tile,), in_specs=[...  94.2 us
    pallas_call x3, Pallas kernels, exchange(): pl.pallas_call(functools.partial(exchange_kernel, steps, 'parts', capacit...  56 us
    psum x1, blocking collectives, on_device(): norms = 0.5 * jnp.log(lax.psum(jnp.stack(partials), 'parts') / scale_total)  39.1 us
    pallas_call x3, Pallas kernels, send_call(): pl.pallas_call(send_kernel, grid=(send_count // send_tile,), in_specs=[wh...  26.1 us

profile of v1, /device:TPU:0, one launch (start us, length us, event | category | flops | bytes accessed | tf_op | source)
XLA Modules:
  0.0 235.6 jit_solution(3581266226409335001)
XLA Ops:
  1.6 0.6 pad_maximum_fusion.3.coef_ref
  2.2 0.6 pad_maximum_fusion.4.coef_ref
  2.8 0.6 pad_maximum_fusion.5.coef_ref
  3.4 0.8 convert_multiply_fusion
  4.2 0.0 copy-start.2
  4.2 0.6 pad_maximum_fusion.1.elem_ref
  4.8 0.7 fusion.22
  5.5 0.7 compare_convert_fusion
  6.2 0.7 fusion.23
  6.9 0.7 fusion.29
  7.7 0.8 reshape.186
  8.5 0.7 add_select_fusion.7
  9.3 0.7 add_select_fusion.4
  10.0 1.0 fusion.7
  11.0 0.7 multiply_select_fusion
  11.8 0.6 pad_maximum_fusion.size_ref
  12.4 0.1 iota_compare_fusion.5
  12.5 0.0 copy-start
  12.5 0.0 copy-start.1
  12.5 0.0 copy-start.3
  12.6 1.0 fusion.4
  13.6 0.0 copy-done.2
  13.6 0.2 and_select_fusion.1
  13.9 0.0 copy-done
  13.9 0.0 copy-done.1
  13.9 0.0 copy-done.3
  13.9 0.7 concatenate.43.code_ref
  14.7 0.1 pad_add_fusion
  14.8 0.6 slice.66.code_ref
  15.4 1.7 copy.23.rows_ref
  17.1 8.7 %send_traces.3 = (f32[72,3584]{1,0:T(8,128)}, bf16[864,512]{1,0:T(8,128)(2,1)}) custom-call(f32[216,512]{1,0:T(8,128)} %dirn_ref.1, f32[1,512]{1,0:T(1,128)} %bitcast.46, s32[3,3584]{1,0:T(4,128)} %slice.66.code_ref, bf16[432,216]{1,0:T(8,128)(2,1)} %constant.150.clone.mat_high, bf16[432,216]{1,0:T(8,128)(2,1)} %constant.151.clone.mat_low, ...), custom_call_target="tpu_custom_call" | custom-call | tf_op jit(solution)/shard_map/send_traces/pallas_call | solution.py:316
  25.7 19.5 %exchange.3.recv_ref = f32[72,3584]{1,0:T(8,128)} custom-call(f32[72,3584]{1,0:T(8,128)} %get-tuple-element.17.src_ref), custom_call_target="tpu_custom_call" | custom-call | tf_op jit(solution)/shard_map/exchange/pallas_call | solution.py:337
  45.3 31.3 %apply_operator.3 = (f32[216,512]{1,0:T(8,128)}, f32[216,512]{1,0:T(8,128)}, f32[2,512]{1,0:T(2,128)}) custom-call(f32[2]{0:T(128)} %pad_maximum_fusion.5.coef_ref, f32[216,512]{1,0:T(8,128)} %dirn_ref.1, f32[216,512]{1,0:T(8,128)} %dirn_ref.1, f32[216,512]{1,0:T(8,128)} %rhs_ref.5, f32[2,512]{1,0:T(2,128)} %pad_maximum_fusion.1.elem_ref, ...), custom_call_target="tpu_custom_call" | custom-call | tf_op jit(solution)/shard_map/apply_operator/pallas_call | solution.py:351
  76.6 0.8 reduce_sum.47
  77.4 8.7 %send_traces.4 = (f32[72,3584]{1,0:T(8,128)}, bf16[864,512]{1,0:T(8,128)(2,1)}) custom-call(f32[216,512]{1,0:T(8,128)} %get-tuple-element.18.x_ref, f32[1,512]{1,0:T(1,128)} %bitcast.47, s32[3,3584]{1,0:T(4,128)} %slice.66.code_ref, bf16[432,216]{1,0:T(8,128)(2,1)} %constant.150.clone.mat_high, bf16[432,216]{1,0:T(8,128)(2,1)} %constant.151.clone.mat_low, ...), custom_call_target="tpu_custom_call" | custom-call | tf_op jit(solution)/shard_map/send_traces/pallas_call | solution.py:316
  86.1 19.1 %exchange.4.recv_ref = f32[72,3584]{1,0:T(8,128)} custom-call(f32[72,3584]{1,0:T(8,128)} %get-tuple-element.21.src_ref), custom_call_target="tpu_custom_call" | custom-call | tf_op jit(solution)/shard_map/exchange/pallas_call | solution.py:337
  105.2 31.4 %apply_operator.4 = (f32[216,512]{1,0:T(8,128)}, f32[216,512]{1,0:T(8,128)}, f32[2,512]{1,0:T(2,128)}) custom-call(f32[2]{0:T(128)} %pad_maximum_fusion.4.coef_ref, f32[216,512]{1,0:T(8,128)} %get-tuple-element.18.x_ref, f32[216,512]{1,0:T(8,128)} %get-tuple-element.19.dirn_ref, f32[216,512]{1,0:T(8,128)} %rhs_ref.5, f32[2,512]{1,0:T(2,128)} %pad_maximum_fusion.1.elem_ref, ...), custom_call_target="tpu_custom_call" | custom-call | tf_op jit(solution)/shard_map/apply_operator/pallas_call | solution.py:351
  136.5 0.8 reduce_sum.48
  137.3 8.7 %send_traces.5 = (f32[72,3584]{1,0:T(8,128)}, bf16[864,512]{1,0:T(8,128)(2,1)}) custom-call(f32[216,512]{1,0:T(8,128)} %get-tuple-element.22.x_ref, f32[1,512]{1,0:T(1,128)} %bitcast.48, s32[3,3584]{1,0:T(4,128)} %slice.66.code_ref, bf16[432,216]{1,0:T(8,128)(2,1)} %constant.150.clone.mat_high, bf16[432,216]{1,0:T(8,128)(2,1)} %constant.151.clone.mat_low, ...), custom_call_target="tpu_custom_call" | custom-call | tf_op jit(solution)/shard_map/send_traces/pallas_call | solution.py:316
  146.0 17.4 %exchange.5.recv_ref = f32[72,3584]{1,0:T(8,128)} custom-call(f32[72,3584]{1,0:T(8,128)} %get-tuple-element.25.src_ref), custom_call_target="tpu_custom_call" | custom-call | tf_op jit(solution)/shard_map/exchange/pallas_call | solution.py:337
  163.5 31.6 %apply_operator.5 = (f32[216,512]{1,0:T(8,128)}, f32[216,512]{1,0:T(8,128)}, f32[2,512]{1,0:T(2,128)}) custom-call(f32[2]{0:T(128)} %pad_maximum_fusion.3.coef_ref, f32[216,512]{1,0:T(8,128)} %get-tuple-element.22.x_ref, f32[216,512]{1,0:T(8,128)} %get-tuple-element.23.dirn_ref, f32[216,512]{1,0:T(8,128)} %rhs_ref.5, f32[2,512]{1,0:T(2,128)} %pad_maximum_fusion.1.elem_ref, ...), custom_call_target="tpu_custom_call" | custom-call | tf_op jit(solution)/shard_map/apply_operator/pallas_call | solution.py:351
  195.0 0.8 reduce_sum.49
  195.8 39.1 %psum.7 = f32[3,2]{1,0:T(4,128)S(1)} all-reduce(f32[3,2]{1,0:T(4,128)S(1)} %pad_maximum_fusion.2), channel_id=1, replica_groups=mesh['parts'=32] {'parts'}, use_global_device_ids=true, to_apply=%region_5.6 | all-reduce | flops 6 | bytes 48 | tf_op jit(solution)/shard_map/psum | solution.py:410
  234.9 0.7 copy.26
  (14 shorter events, 0.2 us)
Async XLA Ops:
  4.2 9.4 %copy-start.2 = (f32[512]{0:T(512)}, f32[512]{0:T(512)S(1)}, u32[]{:S(2)}) copy-start(f32[512]{0:T(512)S(1)} %get-tuple-element.52) | copy-start | bytes 6148
  12.5 1.4 copy-start
  12.5 1.4 copy-start.1
  12.5 1.4 copy-start.3

commit v2 on v1

--- a/solution.py
+++ b/solution.py
@@ -143,10 +143,16 @@
         traces_ref[432:864] = low
 
     code = code_ref[...]
-    out_ref[...] = pick(traces_ref[...], code[0:1], code[1:2], code[2:3], onto_ref[...])
-
-
-def exchange_kernel(steps, axis, capacity, src_ref, dst_ref, send_sem, recv_sem):
+    picked = pick(traces_ref[...], code[0:1], code[1:2], code[2:3], onto_ref[...])
+    capacity = out_ref.shape[2]
+    for k in range(out_ref.shape[0]):
+        out_ref[k] = picked[:, k * capacity : (k + 1) * capacity]
+
+
+def exchange_kernel(
+    steps, axis, width, src_ref, x_ref, traces_ref, code_ref, onto_ref, stiff_high, stiff_low,
+    dst_ref, own_ref, near_ref, volume_ref, send_sem, recv_sem,
+):
     count = lax.axis_size(axis)
     me = lax.axis_index(axis)
     barrier = pltpu.get_barrier_semaphore()
@@ -156,10 +162,9 @@
     pl.semaphore_wait(barrier, len(steps))
     copies = []
     for k, peer in enumerate(peers):
-        part = pl.ds(k * capacity, capacity)
         copy = pltpu.make_async_remote_copy(
-            src_ref=src_ref.at[:, part],
-            dst_ref=dst_ref.at[:, part],
+            src_ref=src_ref.at[k],
+            dst_ref=dst_ref.at[k],
             send_sem=send_sem.at[k],
             recv_sem=recv_sem.at[k],
             device_id=(peer,),
@@ -167,37 +172,86 @@
         )
         copy.start()
         copies.append(copy)
+
+    def step_tile(i, carry):
+        part = pl.ds(pl.multiple_of(i * width, width), width)
+        code = code_ref[:, part]
+        own_ref[:, part] = pick(traces_ref[...], code[0:1], code[1:2], code[2:3], onto_ref[...])
+        near_ref[:, part] = pick(traces_ref[...], code[3:4], code[4:5], code[5:6], onto_ref[...])
+        return carry
+
+    lax.fori_loop(0, code_ref.shape[1] // width, step_tile, 0)
+    volume_ref[...] = dot3(stiff_high[...], stiff_low[...], x_ref[...])
     for copy in copies:
         copy.wait()
 
 
+def norms_kernel(axis, sums_ref, out_ref, landing, send_sem, recv_sem):
+    count = lax.axis_size(axis)
+    me = lax.axis_index(axis)
+    barrier = pltpu.get_barrier_semaphore()
+
+    def greet(k, carry):
+        peer = lax.rem(me + k, count)
+        pl.semaphore_signal(barrier, inc=1, device_id=(peer,), device_id_type=pl.DeviceIdType.MESH)
+        return carry
+
+    def copy_to(k):
+        return pltpu.make_async_remote_copy(
+            src_ref=sums_ref,
+            dst_ref=landing.at[k],
+            send_sem=send_sem.at[k],
+            recv_sem=recv_sem.at[k],
+            device_id=(lax.rem(me + k, count),),
+            device_id_type=pl.DeviceIdType.MESH,
+        )
+
+    def start(k, carry):
+        copy_to(k).start()
+        return carry
+
+    def finish(k, carry):
+        copy_to(k).wait()
+        return carry
+
+    lax.fori_loop(1, count, greet, 0)
+    pl.semaphore_wait(barrier, count - 1)
+    lax.fori_loop(1, count, start, 0)
+    landing[0] = sums_ref[...]
+    lax.fori_loop(1, count, finish, 0)
+
+    def add(j, total):
+        return total + landing[lax.rem(me + count - j, count)]
+
+    total = lax.fori_loop(0, count, add, jnp.zeros(out_ref.shape, F32))
+    out_ref[...] = jnp.broadcast_to(jnp.sum(total, axis=1, keepdims=True), out_ref.shape)
+
+
 def apply_kernel(
-    coef_ref, x_ref, dirn_ref, rhs_ref, elem_ref, prec_ref, traces_ref, recv_ref, code_ref, rows_ref,
-    size_ref, onto_ref, off_ref, weight_ref, stiff_high, stiff_low, lift_high, lift_low,
+    row_index, coef_ref, x_ref, dirn_ref, rhs_ref, elem_ref, prec_ref, recv_ref, own_ref, near_ref,
+    volume_ref, code_ref, rows_ref, size_ref, off_ref, weight_ref, lift_high, lift_low, prior_ref,
     x_out, dirn_out, sums_out, pool, total,
 ):
-    chunk = pool.shape[2]
+    peer_count = recv_ref.shape[0]
 
     @pl.when(pl.program_id(0) == 0)
     def _():
-        for k in range(pool.shape[0]):
-            high, low = split(recv_ref[:, k * chunk : (k + 1) * chunk])
-            pool[k, 0:72] = high
-            pool[k, 72:144] = low
+        for k in range(peer_count):
+            high, low = split(recv_ref[k])
+            pool[144 * k : 144 * k + 72] = high
+            pool[144 * k + 72 : 144 * k + 144] = low
         total[...] = jnp.zeros_like(total)
 
     code = code_ref[...]
-    elem, direction, sub = code[0:1], code[1:2], code[2:3]
-    bound = code[6:7] > 0
-    width = elem.shape[1]
-    own = pick(traces_ref[...], elem, direction, sub, onto_ref[...])
-    near = pick(traces_ref[...], code[3:4], code[4:5], code[5:6], onto_ref[...])
-
-    def far_step(k, carry):
-        return carry + dot(pool[k], one_hot(code[7:8], chunk, k * chunk))
-
-    far = lax.fori_loop(0, pool.shape[0], far_step, jnp.zeros((144, width), F32))
-    partner = near + (far[0:72] + far[72:144])
+    direction, sub = code[1:2], code[2:3]
+    bound = code[6:7] == -1
+    width = sub.shape[1]
+    own = own_ref[...]
+    wide = dot(pool[...], one_hot(code[7:8], pool.shape[1]))
+    partner = near_ref[...]
+    for k in range(peer_count):
+        both = wide[144 * k : 144 * k + 72] + wide[144 * k + 72 : 144 * k + 144]
+        partner = jnp.where(code[6:7] == k, both, partner)
     own_value, own_slope = own[0:36], own[36:72]
     part_value = jnp.where(bound, 0.0, partner[0:36])
     part_slope = jnp.where(bound, -own_slope, partner[36:72])
@@ -213,8 +267,8 @@
     spread_high, spread_low = split(spread)
     back = dot(off_ref[...], jnp.concatenate([spread_high, spread_low, spread_high], axis=0))
     back = jnp.where(sub >= 4, terms, back)
-    wide = jnp.concatenate([jnp.where(direction == d, back, 0.0) for d in range(6)], axis=0)
-    wide_high, wide_low = split(wide)
+    spread = jnp.concatenate([jnp.where(direction == d, back, 0.0) for d in range(6)], axis=0)
+    wide_high, wide_low = split(spread)
     lanes = lax.broadcasted_iota(jnp.int32, (width, total.shape[1]), 1)
     hot = jnp.where(lanes == rows_ref[...], 1.0, 0.0).astype(BF16)
     total[...] += dot(wide_high, hot) + dot(wide_low, hot)
@@ -225,15 +279,19 @@
         field = x_ref[...]
         row = lax.broadcasted_iota(jnp.int32, total.shape, 0)
         faces = jnp.where(lax.rem(row, 72) >= 36, total[...] * inv, total[...])
-        applied = size * dot3(stiff_high[...], stiff_low[...], field)
+        applied = size * volume_ref[...]
         applied = applied + dot3(lift_high[...], lift_low[...], faces)
         residual = jnp.where(size > 0.0, rhs_ref[...] - applied, 0.0)
         scaled = residual * (inv * prec_ref[...])
         step = coef_ref[0] * dirn_ref[...] + coef_ref[1] * scaled
         dirn_out[...] = step
         x_out[...] = field + step
-        sums_out[0:1] = jnp.sum(residual * residual, axis=0, keepdims=True)
-        sums_out[1:2] = jnp.sum(residual * scaled, axis=0, keepdims=True)
+        squares = jnp.sum(residual * residual, axis=0, keepdims=True)
+        products = jnp.sum(residual * scaled, axis=0, keepdims=True)
+        fold = lambda line: sum(line[:, k : k + 128] for k in range(0, line.shape[1], 128))
+        row = lax.broadcasted_iota(jnp.int32, sums_out.shape, 0)
+        later = jnp.where(row == 2 * row_index + 1, fold(products), prior_ref[...])
+        sums_out[...] = jnp.where(row == 2 * row_index, fold(squares), later)
 
 
 def take_small(tables, index):
@@ -275,7 +333,7 @@
     is_remote = jnp.logical_and(jnp.logical_not(is_bound), jnp.logical_not(is_local))
     offset = own_index - rec_peer
     position = jnp.where(offset < 0, offset + far_reach, offset + far_reach - 1)
-    remote_col = jnp.where(is_remote, position * capacity + rec_index, -1)
+    block = jnp.where(is_remote, position, jnp.where(is_bound, -1, -2))
     steps = list(range(-far_reach, 0)) + list(range(1, far_reach + 1))
     lists = send_rec.reshape(part_count, capacity)
     lists = jnp.concatenate([lists[part_count - far_reach :], lists, lists[:far_reach]], axis=0)
@@ -292,7 +350,7 @@
     send_code = found[:, :send_count]
     near = jnp.where(is_local[None], found[:, send_count:], -1)
     rec_code = jnp.concatenate(
-        [jnp.stack([rec_elem, rec_dir, rec_sub]), near, is_bound.astype(jnp.int32)[None], remote_col[None]],
+        [jnp.stack([rec_elem, rec_dir, rec_sub]), near, block[None], rec_index[None]],
         axis=0,
     )
     rec_rows = rec_elem[:, None]
@@ -308,7 +366,7 @@
     prec = jnp.asarray((1.0 / stiff_diag).reshape(216, 1), F32)
     weight = jnp.asarray(face_weight, F32)
 
-    send_tile, rec_tile, chunk = tile(send_count), tile(record_count), tile(send_count)
+    send_tile, rec_tile, peer_count = 2 * capacity, tile(record_count), len(steps)
     params = pltpu.CompilerParams(vmem_limit_bytes=60 * 1024 * 1024)
     field = (216, elem_count)
 
@@ -324,32 +382,60 @@
                 whole((432, 216)),
                 whole((288, 216)),
             ],
-            out_specs=[pl.BlockSpec((72, send_tile), lambda i: (0, i)), whole((864, elem_count))],
+            out_specs=[pl.BlockSpec((2, 72, capacity), lambda i: (i, 0, 0)), whole((864, elem_count))],
             out_shape=[
-                jax.ShapeDtypeStruct((72, send_count), F32),
+                jax.ShapeDtypeStruct((peer_count, 72, capacity), F32),
                 jax.ShapeDtypeStruct((864, elem_count), BF16),
             ],
             compiler_params=params,
             name="send_traces",
         )(x, inv_size[None], send_code, jnp.asarray(mat_high), jnp.asarray(mat_low), jnp.asarray(onto))
 
-    def exchange(outgoing):
+    vmem = pl.BlockSpec(memory_space=pltpu.VMEM)
+
+    def exchange(outgoing, x, element_traces):
         return pl.pallas_call(
-            functools.partial(exchange_kernel, steps, "parts", capacity),
-            in_specs=[pl.BlockSpec(memory_space=pl.ANY)],
-            out_specs=pl.BlockSpec(memory_space=pl.ANY),
-            out_shape=jax.ShapeDtypeStruct((72, send_count), F32),
+            functools.partial(exchange_kernel, steps, "parts", rec_tile),
+            in_specs=[pl.BlockSpec(memory_space=pl.ANY)] + [vmem] * 6,
+            out_specs=[pl.BlockSpec(memory_space=pl.ANY)] + [vmem] * 3,
+            out_shape=[
+                jax.ShapeDtypeStruct((peer_count, 72, capacity), F32),
+                jax.ShapeDtypeStruct((72, record_count), F32),
+                jax.ShapeDtypeStruct((72, record_count), F32),
+                jax.ShapeDtypeStruct(field, F32),
+            ],
             scratch_shapes=[
-                pltpu.SemaphoreType.DMA((len(steps),)),
-                pltpu.SemaphoreType.DMA((len(steps),)),
-            ],
-            compiler_params=pltpu.CompilerParams(collective_id=0, has_side_effects=True),
+                pltpu.SemaphoreType.DMA((peer_count,)),
+                pltpu.SemaphoreType.DMA((peer_count,)),
+            ],
+            compiler_params=pltpu.CompilerParams(
+                collective_id=0, has_side_effects=True, vmem_limit_bytes=60 * 1024 * 1024
+            ),
             name="exchange",
-        )(outgoing)
-
-    def apply_call(coef, x, dirn, element_traces, received):
+        )(
+            outgoing, x, element_traces, rec_code, jnp.asarray(onto),
+            jnp.asarray(stiff_high), jnp.asarray(stiff_low),
+        )
+
+    def all_sums(sums):
         return pl.pallas_call(
-            apply_kernel,
+            functools.partial(norms_kernel, "parts"),
+            in_specs=[vmem],
+            out_specs=vmem,
+            out_shape=jax.ShapeDtypeStruct((8, 128), F32),
+            scratch_shapes=[
+                pltpu.VMEM((part_count, 8, 128), F32),
+                pltpu.SemaphoreType.DMA((part_count,)),
+                pltpu.SemaphoreType.DMA((part_count,)),
+            ],
+            compiler_params=pltpu.CompilerParams(collective_id=1, has_side_effects=True),
+            name="all_sums",
+        )(sums)
+
+    def apply_call(row_index, coef, x, dirn, received, own, near_traces, volume, sums):
+        tiles = lambda rows: pl.BlockSpec((rows, rec_tile), lambda i: (0, i))
+        return pl.pallas_call(
+            functools.partial(apply_kernel, row_index),
             grid=(record_count // rec_tile,),
             in_specs=[
                 pl.BlockSpec(memory_space=pltpu.SMEM),
@@ -358,35 +444,34 @@
                 whole(field),
                 whole((2, elem_count)),
                 whole((216, 1)),
-                whole((864, elem_count)),
-                whole((72, send_count)),
-                pl.BlockSpec((8, rec_tile), lambda i: (0, i)),
+                whole((peer_count, 72, capacity)),
+                tiles(72),
+                tiles(72),
+                whole(field),
+                tiles(8),
                 pl.BlockSpec((rec_tile, 1), lambda i: (i, 0)),
-                pl.BlockSpec((2, rec_tile), lambda i: (0, i)),
-                whole((288, 216)),
+                tiles(2),
                 whole((72, 864)),
                 whole((36, 1)),
-                whole((216, 216)),
-                whole((216, 216)),
                 whole((216, 432)),
                 whole((216, 432)),
-            ],
-            out_specs=[whole(field), whole(field), whole((2, elem_count))],
+                whole((8, 128)),
+            ],
+            out_specs=[whole(field), whole(field), whole((8, 128))],
             out_shape=[
                 jax.ShapeDtypeStruct(field, F32),
                 jax.ShapeDtypeStruct(field, F32),
-                jax.ShapeDtypeStruct((2, elem_count), F32),
+                jax.ShapeDtypeStruct((8, 128), F32),
             ],
             scratch_shapes=[
-                pltpu.VMEM((send_count // chunk, 144, chunk), BF16),
+                pltpu.VMEM((144 * peer_count, capacity), BF16),
                 pltpu.VMEM((432, elem_count), F32),
             ],
             compiler_params=params,
             name="apply_operator",
         )(
-            coef, x, dirn, rhs, elem_rows, prec, element_traces, received, rec_code, rec_rows, size_rows,
-            jnp.asarray(onto), jnp.asarray(off), weight,
-            jnp.asarray(stiff_high), jnp.asarray(stiff_low), jnp.asarray(lift_high), jnp.asarray(lift_low),
+            coef, x, dirn, rhs, elem_rows, prec, received, own, near_traces, volume, rec_code, rec_rows,
+            size_rows, jnp.asarray(off), weight, jnp.asarray(lift_high), jnp.asarray(lift_low), sums,
         )
 
     scale_total = 216.0 * elem_count * part_count
@@ -397,17 +482,16 @@
     sigma_ratio = center / radius
     rho_prev = 1.0 / sigma_ratio
     coef = jnp.stack([jnp.zeros_like(center), 1.0 / center])
-    x, dirn, partials = start, start, []
+    x, dirn, sums = start, start, jnp.zeros((8, 128), F32)
     for step_index in range(ITERS):
         if step_index:
             rho_next = 1.0 / (2.0 * sigma_ratio - rho_prev)
             coef = jnp.stack([rho_next * rho_prev, 2.0 * rho_next / radius])
             rho_prev = rho_next
         outgoing, element_traces = send_call(x)
-        received = exchange(outgoing)
-        x, dirn, sums = apply_call(coef, x, dirn, element_traces, received)
-        partials.append(jnp.sum(sums, axis=1))
-    norms = 0.5 * jnp.log(lax.psum(jnp.stack(partials), "parts") / scale_total)
+        moved = exchange(outgoing, x, element_traces)
+        x, dirn, sums = apply_call(step_index, coef, x, dirn, *moved, sums)
+    norms = 0.5 * jnp.log(all_sums(sums)[: 2 * ITERS, 0].reshape(ITERS, 2) / scale_total)
     return (x, norms)
 
 

time: 237 us -> 168 us (0.71)
  blocking collectives: 39.1 us -> 0 us
  Pallas kernels: 176 us -> 147 us
    psum x1 -> x0, blocking collectives: 39.1 us -> none  [on_device(): norms = 0.5 * jnp.log(lax.psum(jnp.stack(partials), 'parts') / scale_total)]
    pallas_call x6 -> x7, Pallas kernels: 150 us -> 121 us  [the longest x3 64.3 us: exchange(): pl.pallas_call(functools.partial(exchange_kernel, steps, 'parts', rec_til...]
    reduce_sum x3 -> x0, other arithmetic: 2.4 us -> none  [on_device(): partials.append(jnp.sum(sums, axis=1))]
where the time goes in v2:
time: 168 us; the launch traced here: 167 us
  Pallas kernels  147 us (88%)
  other arithmetic  9.49 us (6%)
  local copies, waits for them, and re-layouts  6.64 us (4%)
  matrix products  2.07 us (1%)
  between operations  1.78 us (1%)
    pallas_call x3, Pallas kernels, exchange(): pl.pallas_call(functools.partial(exchange_kernel, steps, 'parts', rec_til...  64.3 us
    pallas_call x3, Pallas kernels, apply_call(): pl.pallas_call(functools.partial(apply_kernel, row_index), grid=(record_c...  45.9 us
    pallas_call x3, Pallas kernels, send_call(): pl.pallas_call(send_kernel, grid=(send_count // send_tile,), in_specs=[wh...  26 us
    pallas_call x1, Pallas kernels, all_sums(): pl.pallas_call(functools.partial(norms_kernel, 'parts'), in_specs=[vmem],...  10.7 us

profile of v2, /device:TPU:0, one launch (start us, length us, event | category | flops | bytes accessed | tf_op | source)
XLA Modules:
  0.0 166.9 jit_solution(2569852053616852041)
XLA Ops:
  1.6 0.6 pad_maximum_fusion.2.coef_ref
  2.2 0.6 pad_maximum_fusion.3.coef_ref
  2.8 0.7 pad_maximum_fusion.4.coef_ref
  3.5 0.7 broadcast_compare_fusion
  4.2 0.8 convert_multiply_fusion
  4.9 0.0 copy-start.2
  4.9 0.6 pad_maximum_fusion.1.elem_ref
  5.5 0.7 fusion.22
  6.3 0.7 select_select_fusion
  7.0 0.7 compare_convert_fusion
  7.7 0.7 fusion.28
  8.4 0.8 reshape.191
  9.3 0.7 constant_dynamic-update-slice_fusion
  10.0 0.7 add_select_fusion.4
  10.8 1.0 fusion.7
  11.8 0.7 multiply_select_fusion
  12.5 0.6 pad_maximum_fusion.size_ref
  13.2 0.1 iota_compare_fusion.5
  13.3 0.0 copy-start
  13.3 0.0 copy-start.1
  13.3 0.0 copy-start.3
  13.3 0.0 copy-start.4
  13.3 1.0 fusion.4
  14.3 0.0 copy-done.2
  14.4 0.2 and_select_fusion.1
  14.6 0.1 pad_add_fusion
  14.7 0.6 slice.70.code_ref
  15.4 0.0 copy-done
  15.4 0.0 copy-done.1
  15.4 0.0 copy-done.3
  15.4 0.0 copy-done.4
  15.4 0.7 concatenate.46.code_ref
  16.1 1.7 %copy.23.rows_ref = s32[3072,1]{1,0:T(8,128)} copy(s32[3072,1]{0,1:T(1,128)S(1)} %bitcast.41) | data formatting | bytes 24576 | tf_op jit(solution)/shard_map/broadcast_in_dim | solution.py:356
  17.8 8.7 %send_traces.3 = (f32[14,72,256]{2,1,0:T(8,128)}, bf16[864,512]{1,0:T(8,128)(2,1)}) custom-call(f32[216,512]{1,0:T(8,128)} %dirn_ref.1, f32[1,512]{1,0:T(1,128)} %bitcast.43, s32[3,3584]{1,0:T(4,128)} %slice.70.code_ref, bf16[432,216]{1,0:T(8,128)(2,1)} %constant.152.clone.mat_high, bf16[432,216]{1,0:T(8,128)(2,1)} %constant.153.clone.mat_low, ...), custom_call_target="tpu_custom_call" | custom-call | tf_op jit(solution)/shard_map/send_traces/pallas_call | solution.py:374
  26.5 22.3 %exchange.3 = (f32[14,72,256]{2,1,0:T(8,128)}, f32[72,3072]{1,0:T(8,128)}, f32[72,3072]{1,0:T(8,128)}, f32[216,512]{1,0:T(8,128)}) custom-call(f32[14,72,256]{2,1,0:T(8,128)} %get-tuple-element.28.src_ref, f32[216,512]{1,0:T(8,128)} %dirn_ref.1, bf16[864,512]{1,0:T(8,128)(2,1)} %get-tuple-element.29.traces_ref, s32[8,3072]{1,0:T(8,128)} %concatenate.46.code_ref, ...), custom_call_target="tpu_custom_call" | custom-call | tf_op jit(solution)/shard_map/exchange/pallas_call | solution.py:397
  48.8 0.6 broadcast_in_dim.71.prior_ref
  49.4 15.2 %apply_operator.3 = (f32[216,512]{1,0:T(8,128)}, f32[216,512]{1,0:T(8,128)}, f32[8,128]{1,0:T(8,128)}) custom-call(f32[2]{0:T(128)} %pad_maximum_fusion.4.coef_ref, f32[216,512]{1,0:T(8,128)} %dirn_ref.1, f32[216,512]{1,0:T(8,128)} %dirn_ref.1, f32[216,512]{1,0:T(8,128)} %rhs_ref.5, f32[2,512]{1,0:T(2,128)} %pad_maximum_fusion.1.elem_ref, ...), custom_call_target="tpu_custom_call" | custom-call | tf_op jit(solution)/shard_map/apply_operator/pallas_call | solution.py:437
  64.6 8.7 %send_traces.4 = (f32[14,72,256]{2,1,0:T(8,128)}, bf16[864,512]{1,0:T(8,128)(2,1)}) custom-call(f32[216,512]{1,0:T(8,128)} %get-tuple-element.34.x_ref, f32[1,512]{1,0:T(1,128)} %bitcast.44, s32[3,3584]{1,0:T(4,128)} %slice.70.code_ref, bf16[432,216]{1,0:T(8,128)(2,1)} %constant.152.clone.mat_high, bf16[432,216]{1,0:T(8,128)(2,1)} %constant.153.clone.mat_low, ...), custom_call_target="tpu_custom_call" | custom-call | tf_op jit(solution)/shard_map/send_traces/pallas_call | solution.py:374
  73.2 21.8 %exchange.4 = (f32[14,72,256]{2,1,0:T(8,128)}, f32[72,3072]{1,0:T(8,128)}, f32[72,3072]{1,0:T(8,128)}, f32[216,512]{1,0:T(8,128)}) custom-call(f32[14,72,256]{2,1,0:T(8,128)} %get-tuple-element.36.src_ref, f32[216,512]{1,0:T(8,128)} %get-tuple-element.34.x_ref, bf16[864,512]{1,0:T(8,128)(2,1)} %get-tuple-element.37.traces_ref, ...), custom_call_target="tpu_custom_call" | custom-call | tf_op jit(solution)/shard_map/exchange/pallas_call | solution.py:397
  95.0 15.3 %apply_operator.4 = (f32[216,512]{1,0:T(8,128)}, f32[216,512]{1,0:T(8,128)}, f32[8,128]{1,0:T(8,128)}) custom-call(f32[2]{0:T(128)} %pad_maximum_fusion.3.coef_ref, f32[216,512]{1,0:T(8,128)} %get-tuple-element.34.x_ref, f32[216,512]{1,0:T(8,128)} %get-tuple-element.35.dirn_ref, f32[216,512]{1,0:T(8,128)} %rhs_ref.5, f32[2,512]{1,0:T(2,128)} %pad_maximum_fusion.1.elem_ref, ...), custom_call_target="tpu_custom_call" | custom-call | tf_op jit(solution)/shard_map/apply_operator/pallas_call | solution.py:437
  110.3 8.7 %send_traces.5 = (f32[14,72,256]{2,1,0:T(8,128)}, bf16[864,512]{1,0:T(8,128)(2,1)}) custom-call(f32[216,512]{1,0:T(8,128)} %get-tuple-element.43.x_ref, f32[1,512]{1,0:T(1,128)} %bitcast.45, s32[3,3584]{1,0:T(4,128)} %slice.70.code_ref, bf16[432,216]{1,0:T(8,128)(2,1)} %constant.152.clone.mat_high, bf16[432,216]{1,0:T(8,128)(2,1)} %constant.153.clone.mat_low, ...), custom_call_target="tpu_custom_call" | custom-call | tf_op jit(solution)/shard_map/send_traces/pallas_call | solution.py:374
  119.0 20.2 %exchange.5 = (f32[14,72,256]{2,1,0:T(8,128)}, f32[72,3072]{1,0:T(8,128)}, f32[72,3072]{1,0:T(8,128)}, f32[216,512]{1,0:T(8,128)}) custom-call(f32[14,72,256]{2,1,0:T(8,128)} %get-tuple-element.45.src_ref, f32[216,512]{1,0:T(8,128)} %get-tuple-element.43.x_ref, bf16[864,512]{1,0:T(8,128)(2,1)} %get-tuple-element.46.traces_ref, ...), custom_call_target="tpu_custom_call" | custom-call | tf_op jit(solution)/shard_map/exchange/pallas_call | solution.py:397
  139.2 15.4 %apply_operator.5 = (f32[216,512]{1,0:T(8,128)}, f32[216,512]{1,0:T(8,128)}, f32[8,128]{1,0:T(8,128)}) custom-call(f32[2]{0:T(128)} %pad_maximum_fusion.2.coef_ref, f32[216,512]{1,0:T(8,128)} %get-tuple-element.43.x_ref, f32[216,512]{1,0:T(8,128)} %get-tuple-element.44.dirn_ref, f32[216,512]{1,0:T(8,128)} %rhs_ref.5, f32[2,512]{1,0:T(2,128)} %pad_maximum_fusion.1.elem_ref, ...), custom_call_target="tpu_custom_call" | custom-call | tf_op jit(solution)/shard_map/apply_operator/pallas_call | solution.py:437
  154.6 10.7 %all_sums.1 = f32[8,128]{1,0:T(8,128)} custom-call(f32[8,128]{1,0:T(8,128)} %get-tuple-element.53.sums_ref), custom_call_target="tpu_custom_call" | custom-call | tf_op jit(solution)/shard_map/all_sums/pallas_call | solution.py:421
  165.4 0.8 multiply_reduce_fusion
  166.1 0.1 mul.69
  166.2 0.7 copy.26
  (12 shorter events, 0.2 us)
Async XLA Ops:
  4.9 9.4 %copy-start.2 = (f32[512]{0:T(512)}, f32[512]{0:T(512)S(1)}, u32[]{:S(2)}) copy-start(f32[512]{0:T(512)S(1)} %get-tuple-element.72) | copy-start | bytes 6148
  13.3 2.1 %copy-start = (s32[3072]{0:T(1024)S(1)}, s32[3072]{0:T(1024)}, u32[]{:S(2)}) copy-start(s32[3072]{0:T(1024)} %param.26) | copy-start | bytes 36868
  13.3 2.1 %copy-start.1 = (s32[3072]{0:T(1024)S(1)}, s32[3072]{0:T(1024)}, u32[]{:S(2)}) copy-start(s32[3072]{0:T(1024)} %param.24) | copy-start | bytes 36868
  13.3 2.1 %copy-start.3 = (s32[3072]{0:T(1024)S(1)}, s32[3072]{0:T(1024)}, u32[]{:S(2)}) copy-start(s32[3072]{0:T(1024)} %param.28) | copy-start | bytes 36868
  13.3 2.1 %copy-start.4 = (s32[3072]{0:T(1024)S(1)}, s32[3072]{0:T(1024)}, u32[]{:S(2)}) copy-start(s32[3072]{0:T(1024)} %param.25) | copy-start | bytes 36868
